TPU v7x, 256 devices: a whole 4x4x8 slice. The times are simulated.
256 devices in a mesh: lon: 16 (over z, x_hi), lat: 16 (over x_lo, y, core).
Axes of the slice: x: 4 (x_hi: 2, x_lo: 2; x = x_hi * 2 + x_lo), y: 4, z: 8, core: 2. Of those that a mesh axis runs over, the one named last changes fastest.
Arguments:
- thermal_departure: float32 [6, 3072, 4096], P(None, 'lat', 'lon'), may hold values from -6 to 6
- saltiness_departure: float32 [6, 3072, 4096], P(None, 'lat', 'lon'), may hold values from -6 to 6
- eastern_edge_speed: float32 [6, 3072, 4096], P(None, 'lat', 'lon'), may hold values from -3 to 3
- northern_edge_speed: float32 [6, 3072, 4096], P(None, 'lat', 'lon'), may hold values from -3 to 3
- water_land_indicator: int32 [6, 3072, 4096], P(None, 'lat', 'lon'), may hold values 0 or 1
Outputs:
- temperature_next: float32 [6, 3072, 4096], P(None, 'lat', 'lon')
- salinity_next: float32 [6, 3072, 4096], P(None, 'lat', 'lon')
- u_next: float32 [6, 3072, 4096], P(None, 'lat', 'lon')
- v_next: float32 [6, 3072, 4096], P(None, 'lat', 'lon')
Inputs may be any that keep to these rules, and one draw needn't show every extreme that they name: `water_land_indicator`: 1 marks a sea cell, 0 a land cell.
All inputs are finite; a program needn't handle non-finite values. No bound on the sum of `water_land_indicator` on one device may be relied on, other than what follows from the above.
Results may differ from a plain program's by a relative error of at most 0.00002.
Values sent between devices are 32-bit elements; how exact they have to be, the bound alone decides.
A program may use at most 128 MiB of HBM per device.

v0:
```python
import jax
import jax.numpy as jnp
from jax import lax
from jax.sharding import PartitionSpec as P

STEPS = 2


time_step = 0.2


def swapped(shard, axis, distance):
    return lax.ppermute(shard, axis, [(i, i ^ 1 << distance) for i in range(lax.axis_size(axis))])


def padded_2(shard, sides, width, wrap):
    for axis, dim in sides:
        size, length = (lax.axis_size(axis), shard.shape[dim])
        up = [(i, (i + 1) % size) for i in range(size if wrap else size - 1)]
        down = [(j, i) for i, j in up]
        last = lax.slice_in_dim(shard, length - width, length, axis=dim)
        initial = lax.slice_in_dim(shard, 0, width, axis=dim)
        before = lax.ppermute(last, axis, up)
        after = lax.ppermute(initial, axis, down)
        shard = jnp.concatenate([before, shard, after], axis=dim)
    return shard


def face_flux(before, centre, after, beyond, velocity):
    return (
        velocity * (7.0 * (centre + after) - (before + beyond)) / 12.0
        - jnp.abs(velocity) * (3.0 * (after - centre) - (beyond - before)) / 12.0
    )


def mirror_rows(rows):
    bit_total = lax.axis_size("lon").bit_length() - 1
    partner = rows
    for bit_number in range(bit_total):
        partner = swapped(partner, "lon", bit_number)
    return partner[..., ::-1]


def east_extend(joined_tracer_planes):
    return padded_2(joined_tracer_planes, (("lon", 3),), 2, True)


def north_extend(joined_tracer_planes, parity):
    row_count = joined_tracer_planes.shape[2]
    padded = padded_2(joined_tracer_planes, (("lat", 2),), 2, False)
    top_rows = (
        jnp.stack(
            [joined_tracer_planes[:, :, row_count - 1], joined_tracer_planes[:, :, row_count - 2]],
            axis=2,
        )
        * parity[:, None, None, None]
    )
    mirror = mirror_rows(top_rows)
    on_top = lax.axis_index("lat") == lax.axis_size("lat") - 1
    ghost_rows = jnp.where(on_top, mirror, padded[:, :, row_count + 2 :])
    return jnp.concatenate([padded[:, :, : row_count + 2], ghost_rows], axis=2)


def advance(joined_tracer_planes, wet, wet_east, wet_north, parity):
    col_count = joined_tracer_planes.shape[3]
    row_count = joined_tracer_planes.shape[2]
    east = east_extend(joined_tracer_planes)
    centre = east[..., 1 : col_count + 2]
    flux = face_flux(
        east[..., 0 : col_count + 1],
        centre,
        east[..., 2 : col_count + 3],
        east[..., 3 : col_count + 4],
        centre[2:3],
    )
    flux = flux * (wet_east[..., 1 : col_count + 2] * wet_east[..., 2 : col_count + 3])
    div_east = flux[..., 1:] - flux[..., :-1]
    north = north_extend(joined_tracer_planes, parity)
    centre = north[:, :, 1 : row_count + 2]
    flux = face_flux(
        north[:, :, 0 : row_count + 1],
        centre,
        north[:, :, 2 : row_count + 3],
        north[:, :, 3 : row_count + 4],
        centre[3:4],
    )
    flux = flux * (wet_north[:, :, 1 : row_count + 2] * wet_north[:, :, 2 : row_count + 3])
    div_north = flux[:, :, 1:] - flux[:, :, :-1]
    return (joined_tracer_planes - time_step * (div_east + div_north)) * wet


def local(
    thermal_departure,
    saltiness_departure,
    eastern_edge_speed,
    northern_edge_speed,
    water_land_indicator,
):
    wet = water_land_indicator.astype(jnp.float32)[None]
    parity = jnp.array([1.0, 1.0, -1.0, -1.0], jnp.float32)
    joined_tracer_planes = jnp.stack(
        [thermal_departure, saltiness_departure, eastern_edge_speed, northern_edge_speed]
    )
    wet_east = east_extend(wet)
    wet_north = north_extend(wet, jnp.ones((1,), jnp.float32))
    for turn in range(STEPS):
        joined_tracer_planes = advance(joined_tracer_planes, wet, wet_east, wet_north, parity)
    return (
        joined_tracer_planes[0],
        joined_tracer_planes[1],
        joined_tracer_planes[2],
        joined_tracer_planes[3],
    )


def solution(mesh):
    placed = (
        P(None, "lat", "lon"),
        P(None, "lat", "lon"),
        P(None, "lat", "lon"),
        P(None, "lat", "lon"),
        P(None, "lat", "lon"),
    )
    return jax.shard_map(
        local,
        mesh=mesh,
        in_specs=placed,
        out_specs=(
            P(None, "lat", "lon"),
            P(None, "lat", "lon"),
            P(None, "lat", "lon"),
            P(None, "lat", "lon"),
        ),
        check_vma=False,
    )
```

profile of v0, /device:TPU:25, one launch (start us, length us, event | category | flops | bytes accessed | tf_op | source)
XLA Modules:
  0.0 193.9 jit_solution(11210959380290086235)
XLA Ops:
  0.7 2.6 %fusion.18 = (f32[6,192,256]{2,1,0:T(8,128)}, f32[1,6,192,256]{3,2,1,0:T(8,128)S(1)}) fusion(s32[6,192,256]{2,1,0:T(8,128)} %param.10), kind=kLoop, calls=%fused_computation.62 | loop fusion | flops 294912 | bytes 3538944 | tf_op jit(solution)/shard_map/convert_element_type | solution.py:99
  3.3 2.8 %collective-permute-start.11 = (f32[1,6,2,256]{3,2,1,0:T(2,128)S(1)}, f32[1,6,2,256]{3,2,1,0:T(2,128)}, u32[]{:S(2)}, u32[]{:S(2)}) collective-permute-start(f32[1,6,2,256]{3,2,1,0:T(2,128)S(1)} %pad_maximum_fusion.15), channel_id=1, source_target_pairs={{0,16},{16,0},{32,48},{48,32},{64,80},{80,64},{96,112},{112,96},{1... | collective-permute-start | bytes 36872 | tf_op jit(solution)/shard_map/ppermute | solution.py:13
  6.7 2.7 %collective-permute-start.10 = (f32[1,6,2,256]{3,2,1,0:T(2,128)}, f32[1,6,2,256]{3,2,1,0:T(2,128)}, u32[]{:S(2)}, u32[]{:S(2)}) collective-permute-start(f32[1,6,2,256]{3,2,1,0:T(2,128)} %get-tuple-element.40), channel_id=1, source_target_pairs={{0,1},{1,2},{2,3},{3,4},{4,5},{5,6},{6,7},{7,8},{8,9},{9,10},{10,1... | collective-permute-start | bytes 36872 | tf_op jit(solution)/shard_map/ppermute | solution.py:23
  9.5 2.1 %collective-permute-start.15 = (f32[1,6,2,256]{3,2,1,0:T(2,128)}, f32[1,6,2,256]{3,2,1,0:T(2,128)}, u32[]{:S(2)}, u32[]{:S(2)}) collective-permute-start(f32[1,6,2,256]{3,2,1,0:T(2,128)} %get-tuple-element.41), channel_id=1, source_target_pairs={{1,0},{2,1},{3,2},{4,3},{5,4},{6,5},{7,6},{8,7},{9,8},{10,9},{11,1... | collective-permute-start | bytes 36872 | tf_op jit(solution)/shard_map/ppermute | solution.py:24
  12.7 1.9 copy.56
  14.7 6.9 %collective-permute-start.3 = (f32[1,6,192,2]{2,3,1,0:T(2,128)}, f32[1,6,192,2]{2,3,1,0:T(2,128)}, u32[]{:S(2)}, u32[]{:S(2)}) collective-permute-start(f32[1,6,192,2]{2,3,1,0:T(2,128)} %copy.56), channel_id=1, source_target_pairs={{16,0},{32,16},{48,32},{64,48},{80,64},{96,80},{112,96},{128,112},... | collective-permute-start | bytes 27656 | tf_op jit(solution)/shard_map/ppermute | solution.py:24
  21.5 1.9 copy.54
  23.5 1.7 pad_maximum_fusion.6
  25.9 3.0 %fusion.15 = (f32[4,6,192,2]{3,2,1,0:T(8,128)}, f32[4,6,192,2]{3,2,1,0:T(8,128)}) fusion(f32[4,6,192,256]{3,2,1,0:T(8,128)S(1)} %pad_maximum_fusion.6), kind=kLoop, calls=%fused_computation.59 | loop fusion | bytes 147456 | tf_op jit(solution)/shard_map/slice | solution.py:21
  29.6 3.2 %copy.50 = f32[4,6,192,2]{2,0,3,1:T(4,128)} copy(f32[4,6,192,2]{3,2,1,0:T(8,128)} %get-tuple-element.28) | data formatting | bytes 73728 | tf_op jit(solution)/shard_map/slice | solution.py:21
  32.8 3.2 %copy.52 = f32[4,6,192,2]{2,0,3,1:T(4,128)} copy(f32[4,6,192,2]{3,2,1,0:T(8,128)} %get-tuple-element.29) | data formatting | bytes 73728 | tf_op jit(solution)/shard_map/slice | solution.py:22
  36.0 5.1 %collective-permute-start.1 = (f32[4,6,192,2]{2,0,3,1:T(4,128)}, f32[4,6,192,2]{2,0,3,1:T(4,128)}, u32[]{:S(2)}, u32[]{:S(2)}) collective-permute-start(f32[4,6,192,2]{2,0,3,1:T(4,128)} %copy.52), channel_id=1, source_target_pairs={{16,0},{32,16},{48,32},{64,48},{80,64},{96,80},{112,96},{128,112},... | collective-permute-start | bytes 110600 | tf_op jit(solution)/shard_map/ppermute | solution.py:24
  41.1 1.8 copy.55
  42.9 1.8 copy.57
  44.6 4.0 %fusion.9 = f32[6,192,257]{2,1,0:T(8,128)} fusion(f32[1,6,192,2]{3,2,1,0:T(8,128)} %copy.57, f32[1,6,192,256]{3,2,1,0:T(8,128)} %copy-done.8, f32[1,6,192,2]{3,2,1,0:T(8,128)} %copy.55), kind=kLoop, calls=%fused_computation.32 | loop fusion | flops 888192 | bytes 2382336 | tf_op jit(solution)/shard_map/mul | solution.py:76
  49.7 3.0 %copy.51 = f32[4,6,192,2]{3,2,1,0:T(8,128)} copy(f32[4,6,192,2]{2,0,3,1:T(4,128)} %collective-permute-done) | data formatting | bytes 73728 | tf_op jit(solution)/shard_map/ppermute | solution.py:23
  52.7 7.1 %collective-permute-start.4 = (f32[4,6,2,256]{3,2,1,0:T(2,128)}, f32[4,6,2,256]{3,2,1,0:T(2,128)}, u32[]{:S(2)}, u32[]{:S(2)}) collective-permute-start(f32[4,6,2,256]{3,2,1,0:T(2,128)} %get-tuple-element.32), channel_id=1, source_target_pairs={{0,1},{1,2},{2,3},{3,4},{4,5},{5,6},{6,7},{7,8},{8,9},{9,10},{10,1... | collective-permute-start | bytes 147464 | tf_op jit(solution)/shard_map/ppermute | solution.py:23
  59.8 3.3 %collective-permute-start.13 = (f32[1,6,2,256]{3,2,1,0:T(2,128)S(1)}, f32[1,6,2,256]{3,2,1,0:T(2,128)}, u32[]{:S(2)}, u32[]{:S(2)}) collective-permute-start(f32[1,6,2,256]{3,2,1,0:T(2,128)S(1)} %collective-permute-done.12), channel_id=1, source_target_pairs={{0,64},{16,80},{32,96},{48,112},{64,0},{80,16},{96,32},{112,48},{1... | collective-permute-start | bytes 36872 | tf_op jit(solution)/shard_map/ppermute | solution.py:13
  63.2 3.0 %copy.53 = f32[4,6,192,2]{3,2,1,0:T(8,128)} copy(f32[4,6,192,2]{2,0,3,1:T(4,128)} %collective-permute-done.1) | data formatting | bytes 73728 | tf_op jit(solution)/shard_map/ppermute | solution.py:24
  66.2 8.7 %maximum_maximum_fusion = (f32[4,6,192,258]{3,2,1,0:T(8,128)S(1)}, f32[4,6,192,258]{3,2,1,0:T(8,128)}) fusion(f32[1,6,192,256]{3,2,1,0:T(8,128)S(1)} %bitcast.35, f32[1,6,192,256]{3,2,1,0:T(8,128)S(1)} %bitcast.41, f32[1,6,192,256]{3,2,1,0:T(8,128)S(1)} %bitcast.47, f32[1,6,192,256]{3,2,1,0:T(8,128)} %bitcast.53, f32[4,6,192,2]{3,2,1,0:T(8,128)} %copy.51, ...), kind=kLoop, calls=%fused_computation.4 | loop fusion | flops 9510912 | bytes 14303232 | tf_op jit(solution)/shard_map/concatenate | solution.py:25
  74.9 2.5 %abs_bitcast_fusion.1 = (f32[6,192,257]{2,1,0:T(8,128)}, f32[1,6,192,257]{3,2,1,0:T(8,128)}) fusion(f32[1,6,192,256]{3,2,1,0:T(8,128)S(1)} %bitcast.36, f32[1,6,192,256]{3,2,1,0:T(8,128)S(1)} %bitcast.42, f32[1,6,192,256]{3,2,1,0:T(8,128)S(1)} %bitcast.48, f32[1,6,192,256]{3,2,1,0:T(8,128)S(1)} %bitcast.56, f32[4,6,192,2]{3,2,1,0:T(8,128)S(1)} %copy-done.7), kind=kLoop, calls=%fused_computation.36 | loop fusion | flops 1480320 | bytes 7123968 | tf_op jit(solution)/shard_map/mul | solution.py:32
  77.4 4.2 %collective-permute-start.14 = (f32[1,6,2,256]{3,2,1,0:T(2,128)}, f32[1,6,2,256]{3,2,1,0:T(2,128)S(1)}, u32[]{:S(2)}, u32[]{:S(2)}) collective-permute-start(f32[1,6,2,256]{3,2,1,0:T(2,128)} %collective-permute-done.13), channel_id=1, source_target_pairs={{0,128},{16,144},{32,160},{48,176},{64,192},{80,208},{96,224},{112... | collective-permute-start | bytes 36872 | tf_op jit(solution)/shard_map/ppermute | solution.py:13
  81.6 10.2 %subtract_multiply_fusion.1 = f32[4,6,192,257]{3,2,1,0:T(8,128)} fusion(f32[4,6,192,258]{3,2,1,0:T(8,128)} %get-tuple-element.27, f32[4,6,192,258]{3,2,1,0:T(8,128)S(1)} %get-tuple-element.26, f32[6,192,257]{2,1,0:T(8,128)} %fusion.9, f32[6,192,257]{2,1,0:T(8,128)} %get-tuple-element.12, f32[6,192,257]{2,1,0:T(8,128)} %bitcast.61), kind=kLoop, calls=%fused_computation.7 | loop fusion | flops 16579584 | bytes 27237888 | tf_op jit(solution)/shard_map/mul | solution.py:76
  92.4 1.9 collective-permute-start.9
  96.1 2.3 %collective-permute-done.6 = f32[4,6,2,256]{3,2,1,0:T(2,128)S(1)} collective-permute-done((f32[4,6,2,256]{3,2,1,0:T(2,128)}, f32[4,6,2,256]{3,2,1,0:T(2,128)S(1)}, u32[]{:S(2)}, u32[]{:S(2)}) %collective-permute-start.6) | collective-permute-done | bytes 49184 | tf_op jit(solution)/shard_map/ppermute | solution.py:13
  98.5 2.3 %abs_bitcast_fusion.3 = (f32[6,193,256]{2,1,0:T(8,128)}, f32[1,6,193,256]{3,2,1,0:T(8,128)}) fusion(f32[1,6,192,256]{3,2,1,0:T(8,128)S(1)} %bitcast.37, f32[1,6,192,256]{3,2,1,0:T(8,128)S(1)} %bitcast.43, f32[1,6,192,256]{3,2,1,0:T(8,128)S(1)} %bitcast.49, f32[1,6,192,256]{3,2,1,0:T(8,128)} %bitcast.54, f32[4,6,2,256]{3,2,1,0:T(2,128)} %collective-permute-done.4), kind=kLoop, calls=%fused_computation.44 | loop fusion | flops 1482240 | bytes 7139328 | tf_op jit(solution)/shard_map/mul | solution.py:32
  100.8 3.1 %collective-permute-done.7 = f32[4,6,2,256]{3,2,1,0:T(2,128)S(1)} collective-permute-done((f32[4,6,2,256]{3,2,1,0:T(2,128)S(1)}, f32[4,6,2,256]{3,2,1,0:T(2,128)S(1)}, u32[]{:S(2)}, u32[]{:S(2)}) %collective-permute-start.7) | collective-permute-done | bytes 49184 | tf_op jit(solution)/shard_map/ppermute | solution.py:13
  105.0 1.9 fusion.11
  106.9 3.9 %collective-permute-done.8 = f32[4,6,2,256]{3,2,1,0:T(2,128)} collective-permute-done((f32[4,6,2,256]{3,2,1,0:T(2,128)S(1)}, f32[4,6,2,256]{3,2,1,0:T(2,128)}, u32[]{:S(2)}, u32[]{:S(2)}) %collective-permute-start.8) | collective-permute-done | bytes 49184 | tf_op jit(solution)/shard_map/ppermute | solution.py:13
  110.8 1.6 rev.9
  113.2 3.2 %maximum_maximum_fusion.1 = (f32[4,6,194,256]{3,2,1,0:T(8,128)S(1)}, f32[4,6,194,256]{3,2,1,0:T(8,128)S(1)}) fusion(f32[1,6,192,256]{3,2,1,0:T(8,128)S(1)} %bitcast.38, f32[1,6,192,256]{3,2,1,0:T(8,128)S(1)} %bitcast.44, f32[1,6,192,256]{3,2,1,0:T(8,128)S(1)} %bitcast.50, f32[1,6,192,256]{3,2,1,0:T(8,128)} %bitcast.55, ...), kind=kLoop, calls=%fused_computation.12 | loop fusion | flops 9535488 | bytes 14352384 | tf_op jit(solution)/shard_map/concatenate | solution.py:25
  116.5 4.6 %subtract_multiply_fusion.3 = f32[4,6,193,256]{3,2,1,0:T(8,128)S(1)} fusion(f32[4,6,194,256]{3,2,1,0:T(8,128)S(1)} %get-tuple-element.31, f32[4,6,194,256]{3,2,1,0:T(8,128)S(1)} %get-tuple-element.30, f32[6,193,256]{2,1,0:T(8,128)} %fusion.11, f32[6,193,256]{2,1,0:T(8,128)} %get-tuple-element.14, f32[6,193,256]{2,1,0:T(8,128)} %bitcast.63), kind=kLoop, calls=%fused_computation.15 | loop fusion | flops 16601088 | bytes 27273216 | tf_op jit(solution)/shard_map/mul | solution.py:87
  121.1 3.1 %fusion.7 = f32[4,6,192,256]{3,2,1,0:T(8,128)S(1)} fusion(f32[4,6,193,256]{3,2,1,0:T(8,128)S(1)} %subtract_multiply_fusion.3, f32[4,6,192,257]{3,2,1,0:T(8,128)S(1)} %bitcast.59, f32[6,192,256]{2,1,0:T(8,128)} %get-tuple-element.36, f32[1,6,192,256]{3,2,1,0:T(8,128)S(1)} %bitcast.39, f32[1,6,192,256]{3,2,1,0:T(8,128)S(1)} %bitcast.45, ...), kind=kLoop, calls=%fused_computation.26 | loop fusion | flops 10616832 | bytes 29491200 | tf_op jit(solution)/shard_map/mul | solution.py:89
  124.3 2.7 %fusion.12 = (f32[4,6,192,2]{3,2,1,0:T(8,128)S(1)}, f32[4,6,192,2]{3,2,1,0:T(8,128)}) fusion(f32[4,6,192,256]{3,2,1,0:T(8,128)S(1)} %fusion.7), kind=kLoop, calls=%fused_computation.56 | loop fusion | bytes 147456 | tf_op jit(solution)/shard_map/slice | solution.py:22
  127.3 2.6 %copy.58 = f32[4,6,192,2]{2,0,3,1:T(4,128)S(1)} copy(f32[4,6,192,2]{3,2,1,0:T(8,128)} %get-tuple-element.21) | data formatting | bytes 73728 | tf_op jit(solution)/shard_map/slice | solution.py:21
  129.9 3.2 %collective-permute-start.16 = (f32[4,6,192,2]{2,0,3,1:T(4,128)S(1)}, f32[4,6,192,2]{2,0,3,1:T(4,128)S(1)}, u32[]{:S(2)}, u32[]{:S(2)}) collective-permute-start(f32[4,6,192,2]{2,0,3,1:T(4,128)S(1)} %copy.58), channel_id=1, source_target_pairs={{0,16},{16,32},{32,48},{48,64},{64,80},{80,96},{96,112},{112,128},... | collective-permute-start | bytes 110600 | tf_op jit(solution)/shard_map/ppermute | solution.py:23
  134.2 4.1 %collective-permute-start.23 = (f32[4,6,2,256]{3,2,1,0:T(2,128)S(1)}, f32[4,6,2,256]{3,2,1,0:T(2,128)S(1)}, u32[]{:S(2)}, u32[]{:S(2)}) collective-permute-start(f32[4,6,2,256]{3,2,1,0:T(2,128)S(1)} %get-tuple-element.22), channel_id=1, source_target_pairs={{1,0},{2,1},{3,2},{4,3},{5,4},{6,5},{7,6},{8,7},{9,8},{10,9},{11,1... | collective-permute-start | bytes 147464 | tf_op jit(solution)/shard_map/ppermute | solution.py:24
  138.3 6.6 %collective-permute-start.18 = (f32[4,6,2,256]{3,2,1,0:T(2,128)S(1)}, f32[4,6,2,256]{3,2,1,0:T(2,128)S(1)}, u32[]{:S(2)}, u32[]{:S(2)}) collective-permute-start(f32[4,6,2,256]{3,2,1,0:T(2,128)S(1)} %get-tuple-element.23), channel_id=1, source_target_pairs={{0,1},{1,2},{2,3},{3,4},{4,5},{5,6},{6,7},{7,8},{8,9},{9,10},{10,1... | collective-permute-start | bytes 147464 | tf_op jit(solution)/shard_map/ppermute | solution.py:23
  145.7 2.9 %collective-permute-start.17 = (f32[4,6,192,2]{2,0,3,1:T(4,128)S(1)}, f32[4,6,192,2]{2,0,3,1:T(4,128)S(1)}, u32[]{:S(2)}, u32[]{:S(2)}) collective-permute-start(f32[4,6,192,2]{2,0,3,1:T(4,128)S(1)} %copy.60), channel_id=1, source_target_pairs={{16,0},{32,16},{48,32},{64,48},{80,64},{96,80},{112,96},{128,112},... | collective-permute-start | bytes 110600 | tf_op jit(solution)/shard_map/ppermute | solution.py:24
  149.5 3.7 %abs_bitcast_fusion = (f32[6,192,257]{2,1,0:T(8,128)}, f32[1,6,192,257]{3,2,1,0:T(8,128)}) fusion(f32[4,6,192,256]{3,2,1,0:T(8,128)} %copy-done, f32[4,6,192,2]{3,2,1,0:T(8,128)S(1)} %copy.59), kind=kLoop, calls=%fused_computation.35 | loop fusion | flops 592128 | bytes 7123968 | tf_op jit(solution)/shard_map/mul | solution.py:32
  153.3 2.2 %copy.61 = f32[4,6,192,2]{3,2,1,0:T(8,128)} copy(f32[4,6,192,2]{2,0,3,1:T(4,128)S(1)} %collective-permute-done.17) | data formatting | bytes 73728 | tf_op jit(solution)/shard_map/ppermute | solution.py:24
  155.4 16.2 %subtract_multiply_fusion = f32[4,6,192,257]{3,2,1,0:T(8,128)} fusion(f32[4,6,192,256]{3,2,1,0:T(8,128)} %copy-done, f32[4,6,192,2]{3,2,1,0:T(8,128)S(1)} %copy.59, f32[4,6,192,2]{3,2,1,0:T(8,128)} %copy.61, f32[6,192,257]{2,1,0:T(8,128)} %get-tuple-element.8, f32[6,192,257]{2,1,0:T(8,128)} %bitcast.60, f32[6,192,257]{2,1,0:T(8,128)} %fusion.9), kind=kLoop, calls=%fused_computation.6 | loop fusion | flops 21316608 | bytes 13082112 | tf_op jit(solution)/shard_map/mul | solution.py:76
  171.6 2.2 %collective-permute-start.22 = (f32[4,6,2,256]{3,2,1,0:T(2,128)S(1)}, f32[4,6,2,256]{3,2,1,0:T(2,128)S(1)}, u32[]{:S(2)}, u32[]{:S(2)}) collective-permute-start(f32[4,6,2,256]{3,2,1,0:T(2,128)S(1)} %collective-permute-done.21), channel_id=1, source_target_pairs={{0,128},{16,144},{32,160},{48,176},{64,192},{80,208},{96,224},{112... | collective-permute-start | bytes 147464 | tf_op jit(solution)/shard_map/ppermute | solution.py:13
  173.9 1.7 abs_bitcast_fusion.2
  175.6 3.0 %collective-permute-done.22 = f32[4,6,2,256]{3,2,1,0:T(2,128)S(1)} collective-permute-done((f32[4,6,2,256]{3,2,1,0:T(2,128)S(1)}, f32[4,6,2,256]{3,2,1,0:T(2,128)S(1)}, u32[]{:S(2)}, u32[]{:S(2)}) %collective-permute-start.22) | collective-permute-done | bytes 49184 | tf_op jit(solution)/shard_map/ppermute | solution.py:13
  179.0 9.9 %subtract_multiply_fusion.2 = f32[4,6,193,256]{3,2,1,0:T(8,128)S(1)} fusion(f32[4,6,192,256]{3,2,1,0:T(8,128)} %copy-done, f32[4,6,2,256]{3,2,1,0:T(2,128)S(1)} %collective-permute-done.18, f32[4,6,2,256]{3,2,1,0:T(2,128)S(1)} %broadcast_select_fusion, f32[6,193,256]{2,1,0:T(8,128)} %get-tuple-element.10, f32[6,193,256]{2,1,0:T(8,128)} %bitcast.62, ...), kind=kLoop, calls=%fused_computation.14 | loop fusion | flops 21344256 | bytes 13117440 | tf_op jit(solution)/shard_map/mul | solution.py:87
  189.6 2.0 %fusion.3 = f32[4,6,192,256]{3,2,1,0:T(8,128)S(1)} fusion(f32[4,6,192,256]{3,2,1,0:T(8,128)S(1)} %bitcast.33, f32[4,6,193,256]{3,2,1,0:T(8,128)S(1)} %subtract_multiply_fusion.2, f32[4,6,192,257]{3,2,1,0:T(8,128)S(1)} %copy-done.6, f32[6,192,256]{2,1,0:T(8,128)S(1)} %copy-done.11), kind=kLoop, calls=%fused_computation.20 | loop fusion | flops 7077888 | bytes 29491200 | tf_op jit(solution)/shard_map/mul | solution.py:89
  191.6 2.3 %slice_bitcast_fusion = (f32[6,192,256]{2,1,0:T(8,128)}, f32[6,192,256]{2,1,0:T(8,128)}, f32[6,192,256]{2,1,0:T(8,128)}, f32[6,192,256]{2,1,0:T(8,128)}) fusion(f32[4,6,192,256]{3,2,1,0:T(8,128)S(1)} %fusion.3), kind=kLoop, calls=%fused_computation.45 | loop fusion | bytes 9437184 | tf_op jit(solution)/shard_map/squeeze | solution.py:112
  (90 shorter events, 13.0 us)
Async XLA Ops:
  0.6 22.8 %copy-start.1 = (f32[6,192,256]{2,1,0:T(8,128)S(1)}, f32[6,192,256]{2,1,0:T(8,128)}, u32[]{:S(2)}) copy-start(f32[6,192,256]{2,1,0:T(8,128)} %param.9) | copy-start | bytes 3538948
  0.6 22.8 %copy-start.2 = (f32[6,192,256]{2,1,0:T(8,128)S(1)}, f32[6,192,256]{2,1,0:T(8,128)}, u32[]{:S(2)}) copy-start(f32[6,192,256]{2,1,0:T(8,128)} %param.8) | copy-start | bytes 3538948
  0.7 22.8 %copy-start.3 = (f32[6,192,256]{2,1,0:T(8,128)S(1)}, f32[6,192,256]{2,1,0:T(8,128)}, u32[]{:S(2)}) copy-start(f32[6,192,256]{2,1,0:T(8,128)} %param.7) | copy-start | bytes 3538948
  3.3 8.3 %copy-start.8 = (f32[1,6,192,256]{3,2,1,0:T(8,128)}, f32[1,6,192,256]{3,2,1,0:T(8,128)S(1)}, u32[]{:S(2)}) copy-start(f32[1,6,192,256]{3,2,1,0:T(8,128)S(1)} %get-tuple-element.37) | copy-start | bytes 3538948
  3.3 41.4 %collective-permute-start.11 = (f32[1,6,2,256]{3,2,1,0:T(2,128)S(1)}, f32[1,6,2,256]{3,2,1,0:T(2,128)}, u32[]{:S(2)}, u32[]{:S(2)}) collective-permute-start(f32[1,6,2,256]{3,2,1,0:T(2,128)S(1)} %pad_maximum_fusion.15), channel_id=1, source_target_pairs={{0,16},{16,0},{32,48},{48,32},{64,80},{80,64},{96,112},{112,96},{1... | collective-permute-start | bytes 36872 | tf_op jit(solution)/shard_map/ppermute | solution.py:13
  6.7 98.3 %collective-permute-start.10 = (f32[1,6,2,256]{3,2,1,0:T(2,128)}, f32[1,6,2,256]{3,2,1,0:T(2,128)}, u32[]{:S(2)}, u32[]{:S(2)}) collective-permute-start(f32[1,6,2,256]{3,2,1,0:T(2,128)} %get-tuple-element.40), channel_id=1, source_target_pairs={{0,1},{1,2},{2,3},{3,4},{4,5},{5,6},{6,7},{7,8},{8,9},{9,10},{10,1... | collective-permute-start | bytes 36872 | tf_op jit(solution)/shard_map/ppermute | solution.py:23
  9.5 85.9 %collective-permute-start.15 = (f32[1,6,2,256]{3,2,1,0:T(2,128)}, f32[1,6,2,256]{3,2,1,0:T(2,128)}, u32[]{:S(2)}, u32[]{:S(2)}) collective-permute-start(f32[1,6,2,256]{3,2,1,0:T(2,128)} %get-tuple-element.41), channel_id=1, source_target_pairs={{1,0},{2,1},{3,2},{4,3},{5,4},{6,5},{7,6},{8,7},{9,8},{10,9},{11,1... | collective-permute-start | bytes 36872 | tf_op jit(solution)/shard_map/ppermute | solution.py:24
  14.7 28.2 %collective-permute-start.3 = (f32[1,6,192,2]{2,3,1,0:T(2,128)}, f32[1,6,192,2]{2,3,1,0:T(2,128)}, u32[]{:S(2)}, u32[]{:S(2)}) collective-permute-start(f32[1,6,192,2]{2,3,1,0:T(2,128)} %copy.56), channel_id=1, source_target_pairs={{16,0},{32,16},{48,32},{64,48},{80,64},{96,80},{112,96},{128,112},... | collective-permute-start | bytes 27656 | tf_op jit(solution)/shard_map/ppermute | solution.py:24
  23.5 12.5 %collective-permute-start.2 = (f32[1,6,192,2]{2,3,1,0:T(2,128)}, f32[1,6,192,2]{2,3,1,0:T(2,128)}, u32[]{:S(2)}, u32[]{:S(2)}) collective-permute-start(f32[1,6,192,2]{2,3,1,0:T(2,128)} %copy.54), channel_id=1, source_target_pairs={{0,16},{16,32},{32,48},{48,64},{64,80},{80,96},{96,112},{112,128},... | collective-permute-start | bytes 27656 | tf_op jit(solution)/shard_map/ppermute | solution.py:23
  25.9 3.0 %copy-start.13 = (f32[4]{0:T(128)S(1)}, f32[4]{0:T(128)}, u32[]{:S(2)}) copy-start(f32[4]{0:T(128)} %constant.27.clone) | copy-start | bytes 52
  36.0 23.8 %collective-permute-start.1 = (f32[4,6,192,2]{2,0,3,1:T(4,128)}, f32[4,6,192,2]{2,0,3,1:T(4,128)}, u32[]{:S(2)}, u32[]{:S(2)}) collective-permute-start(f32[4,6,192,2]{2,0,3,1:T(4,128)} %copy.52), channel_id=1, source_target_pairs={{16,0},{32,16},{48,32},{64,48},{80,64},{96,80},{112,96},{128,112},... | collective-permute-start | bytes 110600 | tf_op jit(solution)/shard_map/ppermute | solution.py:24
  42.9 6.9 %collective-permute-start = (f32[4,6,192,2]{2,0,3,1:T(4,128)}, f32[4,6,192,2]{2,0,3,1:T(4,128)}, u32[]{:S(2)}, u32[]{:S(2)}) collective-permute-start(f32[4,6,192,2]{2,0,3,1:T(4,128)} %copy.50), channel_id=1, source_target_pairs={{0,16},{16,32},{32,48},{48,64},{64,80},{80,96},{96,112},{112,128},... | collective-permute-start | bytes 110600 | tf_op jit(solution)/shard_map/ppermute | solution.py:23
  44.6 8.1 %collective-permute-start.12 = (f32[1,6,2,256]{3,2,1,0:T(2,128)}, f32[1,6,2,256]{3,2,1,0:T(2,128)S(1)}, u32[]{:S(2)}, u32[]{:S(2)}) collective-permute-start(f32[1,6,2,256]{3,2,1,0:T(2,128)} %collective-permute-done.11), channel_id=1, source_target_pairs={{0,32},{16,48},{32,0},{48,16},{64,96},{80,112},{96,64},{112,80},{1... | collective-permute-start | bytes 36872 | tf_op jit(solution)/shard_map/ppermute | solution.py:13
  49.7 45.5 %collective-permute-start.5 = (f32[4,6,2,256]{3,2,1,0:T(2,128)}, f32[4,6,2,256]{3,2,1,0:T(2,128)}, u32[]{:S(2)}, u32[]{:S(2)}) collective-permute-start(f32[4,6,2,256]{3,2,1,0:T(2,128)} %maximum_multiply_fusion), channel_id=1, source_target_pairs={{0,16},{16,0},{32,48},{48,32},{64,80},{80,64},{96,112},{112,96},{1... | collective-permute-start | bytes 147464 | tf_op jit(solution)/shard_map/ppermute | solution.py:13
  52.7 45.8 %collective-permute-start.4 = (f32[4,6,2,256]{3,2,1,0:T(2,128)}, f32[4,6,2,256]{3,2,1,0:T(2,128)}, u32[]{:S(2)}, u32[]{:S(2)}) collective-permute-start(f32[4,6,2,256]{3,2,1,0:T(2,128)} %get-tuple-element.32), channel_id=1, source_target_pairs={{0,1},{1,2},{2,3},{3,4},{4,5},{5,6},{6,7},{7,8},{8,9},{9,10},{10,1... | collective-permute-start | bytes 147464 | tf_op jit(solution)/shard_map/ppermute | solution.py:23
  59.8 17.5 %collective-permute-start.13 = (f32[1,6,2,256]{3,2,1,0:T(2,128)S(1)}, f32[1,6,2,256]{3,2,1,0:T(2,128)}, u32[]{:S(2)}, u32[]{:S(2)}) collective-permute-start(f32[1,6,2,256]{3,2,1,0:T(2,128)S(1)} %collective-permute-done.12), channel_id=1, source_target_pairs={{0,64},{16,80},{32,96},{48,112},{64,0},{80,16},{96,32},{112,48},{1... | collective-permute-start | bytes 36872 | tf_op jit(solution)/shard_map/ppermute | solution.py:13
  66.2 8.7 %copy-start.4 = (f32[6,192,256]{2,1,0:T(8,128)S(1)}, f32[6,192,256]{2,1,0:T(8,128)}, u32[]{:S(2)}) copy-start(f32[6,192,256]{2,1,0:T(8,128)} %param.6) | copy-start | bytes 3538948
  66.2 8.7 %copy-start.7 = (f32[4,6,192,2]{3,2,1,0:T(8,128)S(1)}, f32[4,6,192,2]{3,2,1,0:T(8,128)}, u32[]{:S(2)}) copy-start(f32[4,6,192,2]{3,2,1,0:T(8,128)} %copy.51) | copy-start | bytes 110596
  77.4 14.4 %collective-permute-start.14 = (f32[1,6,2,256]{3,2,1,0:T(2,128)}, f32[1,6,2,256]{3,2,1,0:T(2,128)S(1)}, u32[]{:S(2)}, u32[]{:S(2)}) collective-permute-start(f32[1,6,2,256]{3,2,1,0:T(2,128)} %collective-permute-done.13), channel_id=1, source_target_pairs={{0,128},{16,144},{32,160},{48,176},{64,192},{80,208},{96,224},{112... | collective-permute-start | bytes 36872 | tf_op jit(solution)/shard_map/ppermute | solution.py:13
  91.8 0.6 copy-start.12
  92.4 20.0 %collective-permute-start.9 = (f32[4,6,2,256]{3,2,1,0:T(2,128)}, f32[4,6,2,256]{3,2,1,0:T(2,128)}, u32[]{:S(2)}, u32[]{:S(2)}) collective-permute-start(f32[4,6,2,256]{3,2,1,0:T(2,128)} %get-tuple-element.33), channel_id=1, source_target_pairs={{1,0},{2,1},{3,2},{4,3},{5,4},{6,5},{7,6},{8,7},{9,8},{10,9},{11,1... | collective-permute-start | bytes 147464 | tf_op jit(solution)/shard_map/ppermute | solution.py:24
  95.2 9.8 %copy-start.9 = (f32[1,6,192,256]{3,2,1,0:T(8,128)S(1)}, f32[1,6,192,256]{3,2,1,0:T(8,128)}, u32[]{:S(2)}) copy-start(f32[1,6,192,256]{3,2,1,0:T(8,128)} %copy-done.8) | copy-start | bytes 3538948
  95.2 3.2 %collective-permute-start.6 = (f32[4,6,2,256]{3,2,1,0:T(2,128)}, f32[4,6,2,256]{3,2,1,0:T(2,128)S(1)}, u32[]{:S(2)}, u32[]{:S(2)}) collective-permute-start(f32[4,6,2,256]{3,2,1,0:T(2,128)} %collective-permute-done.5), channel_id=1, source_target_pairs={{0,32},{16,48},{32,0},{48,16},{64,96},{80,112},{96,64},{112,80},{1... | collective-permute-start | bytes 147464 | tf_op jit(solution)/shard_map/ppermute | solution.py:13
  98.4 5.4 %collective-permute-start.7 = (f32[4,6,2,256]{3,2,1,0:T(2,128)S(1)}, f32[4,6,2,256]{3,2,1,0:T(2,128)S(1)}, u32[]{:S(2)}, u32[]{:S(2)}) collective-permute-start(f32[4,6,2,256]{3,2,1,0:T(2,128)S(1)} %collective-permute-done.6), channel_id=1, source_target_pairs={{0,64},{16,80},{32,96},{48,112},{64,0},{80,16},{96,32},{112,48},{1... | collective-permute-start | bytes 147464 | tf_op jit(solution)/shard_map/ppermute | solution.py:13
  103.8 7.0 %collective-permute-start.8 = (f32[4,6,2,256]{3,2,1,0:T(2,128)S(1)}, f32[4,6,2,256]{3,2,1,0:T(2,128)}, u32[]{:S(2)}, u32[]{:S(2)}) collective-permute-start(f32[4,6,2,256]{3,2,1,0:T(2,128)S(1)} %collective-permute-done.7), channel_id=1, source_target_pairs={{0,128},{16,144},{32,160},{48,176},{64,192},{80,208},{96,224},{112... | collective-permute-start | bytes 147464 | tf_op jit(solution)/shard_map/ppermute | solution.py:13
  113.2 7.9 %slice-start.4 = ((s8[7077888]{0:T(1024)(128)(4,1)}), s8[4194304]{0:T(1024)(128)(4,1)S(1)}, s32[]{:S(2)}) async-start(s8[7077888]{0:T(1024)(128)(4,1)} %bitcast.58), calls=%async_computation.4 | async-start | bytes 8388608
  116.5 4.6 %copy-start.5 = (f32[6,192,256]{2,1,0:T(8,128)S(1)}, f32[6,192,256]{2,1,0:T(8,128)}, u32[]{:S(2)}) copy-start(f32[6,192,256]{2,1,0:T(8,128)} %param.6) | copy-start | bytes 3538948
  116.5 4.6 %slice-start.5 = ((s8[7077888]{0:T(1024)(128)(4,1)}), s8[2883584]{0:T(1024)(128)(4,1)S(1)}, s32[]{:S(2)}) async-start(s8[7077888]{0:T(1024)(128)(4,1)} %bitcast.58), calls=%async_computation.5 | async-start | bytes 5767168
  124.3 2.8 %copy-start = (f32[4,6,192,256]{3,2,1,0:T(8,128)}, f32[4,6,192,256]{3,2,1,0:T(8,128)S(1)}, u32[]{:S(2)}) copy-start(f32[4,6,192,256]{3,2,1,0:T(8,128)S(1)} %fusion.7) | copy-start | bytes 14155780
  127.2 22.2 %collective-permute-start.19 = (f32[4,6,2,256]{3,2,1,0:T(2,128)S(1)}, f32[4,6,2,256]{3,2,1,0:T(2,128)S(1)}, u32[]{:S(2)}, u32[]{:S(2)}) collective-permute-start(f32[4,6,2,256]{3,2,1,0:T(2,128)S(1)} %maximum_multiply_fusion.1), channel_id=1, source_target_pairs={{0,16},{16,0},{32,48},{48,32},{64,80},{80,64},{96,112},{112,96},{1... | collective-permute-start | bytes 147464 | tf_op jit(solution)/shard_map/ppermute | solution.py:13
  129.9 18.8 %collective-permute-start.16 = (f32[4,6,192,2]{2,0,3,1:T(4,128)S(1)}, f32[4,6,192,2]{2,0,3,1:T(4,128)S(1)}, u32[]{:S(2)}, u32[]{:S(2)}) collective-permute-start(f32[4,6,192,2]{2,0,3,1:T(4,128)S(1)} %copy.58), channel_id=1, source_target_pairs={{0,16},{16,32},{32,48},{48,64},{64,80},{80,96},{96,112},{112,128},... | collective-permute-start | bytes 110600 | tf_op jit(solution)/shard_map/ppermute | solution.py:23
  134.2 44.7 %collective-permute-start.23 = (f32[4,6,2,256]{3,2,1,0:T(2,128)S(1)}, f32[4,6,2,256]{3,2,1,0:T(2,128)S(1)}, u32[]{:S(2)}, u32[]{:S(2)}) collective-permute-start(f32[4,6,2,256]{3,2,1,0:T(2,128)S(1)} %get-tuple-element.22), channel_id=1, source_target_pairs={{1,0},{2,1},{3,2},{4,3},{5,4},{6,5},{7,6},{8,7},{9,8},{10,9},{11,1... | collective-permute-start | bytes 147464 | tf_op jit(solution)/shard_map/ppermute | solution.py:24
  138.3 35.6 %collective-permute-start.18 = (f32[4,6,2,256]{3,2,1,0:T(2,128)S(1)}, f32[4,6,2,256]{3,2,1,0:T(2,128)S(1)}, u32[]{:S(2)}, u32[]{:S(2)}) collective-permute-start(f32[4,6,2,256]{3,2,1,0:T(2,128)S(1)} %get-tuple-element.23), channel_id=1, source_target_pairs={{0,1},{1,2},{2,3},{3,4},{4,5},{5,6},{6,7},{7,8},{8,9},{9,10},{10,1... | collective-permute-start | bytes 147464 | tf_op jit(solution)/shard_map/ppermute | solution.py:23
  145.7 7.5 %collective-permute-start.17 = (f32[4,6,192,2]{2,0,3,1:T(4,128)S(1)}, f32[4,6,192,2]{2,0,3,1:T(4,128)S(1)}, u32[]{:S(2)}, u32[]{:S(2)}) collective-permute-start(f32[4,6,192,2]{2,0,3,1:T(4,128)S(1)} %copy.60), channel_id=1, source_target_pairs={{16,0},{32,16},{48,32},{64,48},{80,64},{96,80},{112,96},{128,112},... | collective-permute-start | bytes 110600 | tf_op jit(solution)/shard_map/ppermute | solution.py:24
  149.4 6.0 %collective-permute-start.20 = (f32[4,6,2,256]{3,2,1,0:T(2,128)S(1)}, f32[4,6,2,256]{3,2,1,0:T(2,128)S(1)}, u32[]{:S(2)}, u32[]{:S(2)}) collective-permute-start(f32[4,6,2,256]{3,2,1,0:T(2,128)S(1)} %collective-permute-done.19), channel_id=1, source_target_pairs={{0,32},{16,48},{32,0},{48,16},{64,96},{80,112},{96,64},{112,80},{1... | collective-permute-start | bytes 147464 | tf_op jit(solution)/shard_map/ppermute | solution.py:13
  153.3 20.6 %slice-start = ((s8[4718592]{0:T(1024)(128)(4,1)}), s8[524288]{0:T(1024)(128)(4,1)S(1)}, s32[]{:S(2)}) async-start(s8[4718592]{0:T(1024)(128)(4,1)} %bitcast.30), calls=%async_computation | async-start | bytes 1048576
  155.4 16.2 %collective-permute-start.21 = (f32[4,6,2,256]{3,2,1,0:T(2,128)S(1)}, f32[4,6,2,256]{3,2,1,0:T(2,128)S(1)}, u32[]{:S(2)}, u32[]{:S(2)}) collective-permute-start(f32[4,6,2,256]{3,2,1,0:T(2,128)S(1)} %collective-permute-done.20), channel_id=1, source_target_pairs={{0,64},{16,80},{32,96},{48,112},{64,0},{80,16},{96,32},{112,48},{1... | collective-permute-start | bytes 147464 | tf_op jit(solution)/shard_map/ppermute | solution.py:13
  155.4 18.4 %slice-start.1 = ((s8[4718592]{0:T(1024)(128)(4,1)}), s8[4194304]{0:T(1024)(128)(4,1)S(1)}, s32[]{:S(2)}) async-start(s8[4718592]{0:T(1024)(128)(4,1)} %bitcast.30), calls=%async_computation.1 | async-start | bytes 8388608
  171.6 7.3 %copy-start.10 = (f32[6,193,256]{2,1,0:T(8,128)S(1)}, f32[6,193,256]{2,1,0:T(8,128)}, u32[]{:S(2)}) copy-start(f32[6,193,256]{2,1,0:T(8,128)} %fusion.11) | copy-start | bytes 3557380
  171.6 7.0 %collective-permute-start.22 = (f32[4,6,2,256]{3,2,1,0:T(2,128)S(1)}, f32[4,6,2,256]{3,2,1,0:T(2,128)S(1)}, u32[]{:S(2)}, u32[]{:S(2)}) collective-permute-start(f32[4,6,2,256]{3,2,1,0:T(2,128)S(1)} %collective-permute-done.21), channel_id=1, source_target_pairs={{0,128},{16,144},{32,160},{48,176},{64,192},{80,208},{96,224},{112... | collective-permute-start | bytes 147464 | tf_op jit(solution)/shard_map/ppermute | solution.py:13
  173.9 15.0 %slice-start.2 = ((s8[4718592]{0:T(1024)(128)(4,1)}), s8[524288]{0:T(1024)(128)(4,1)S(1)}, s32[]{:S(2)}) async-start(s8[4718592]{0:T(1024)(128)(4,1)} %bitcast.32), calls=%async_computation.2 | async-start | bytes 1048576
  178.9 9.9 %slice-start.3 = ((s8[4718592]{0:T(1024)(128)(4,1)}), s8[4194304]{0:T(1024)(128)(4,1)S(1)}, s32[]{:S(2)}) async-start(s8[4718592]{0:T(1024)(128)(4,1)} %bitcast.32), calls=%async_computation.3 | async-start | bytes 8388608
  178.9 10.4 %copy-start.6 = (f32[4,6,192,257]{3,2,1,0:T(8,128)S(1)}, f32[4,6,192,257]{3,2,1,0:T(8,128)}, u32[]{:S(2)}) copy-start(f32[4,6,192,257]{3,2,1,0:T(8,128)} %subtract_multiply_fusion) | copy-start | bytes 14211076
  178.9 10.7 %copy-start.11 = (f32[6,192,256]{2,1,0:T(8,128)S(1)}, f32[6,192,256]{2,1,0:T(8,128)}, u32[]{:S(2)}) copy-start(f32[6,192,256]{2,1,0:T(8,128)} %get-tuple-element.36) | copy-start | bytes 3538948
where the time goes:
time: 195 us; the launch traced here: 194 us
  other arithmetic  80.7 us (41%)
  starting transfers between devices  56.6 us (29%)
  local copies, waits for them, and re-layouts  42.1 us (22%)
  waiting for transfers between devices  13.4 us (7%)
    mul x3, other arithmetic, advance(): flux * (wet_east[..., 1:col_count + 2] * wet_east[..., 2:col_count + 3])  30.4 us
    ppermute x6, starting transfers between devices, padded_2(): after = lax.ppermute(initial, axis, down)  22.9 us
    ppermute x6, starting transfers between devices, padded_2(): before = lax.ppermute(last, axis, up)  19.6 us
    mul x3, other arithmetic, advance(): flux * (wet_north[:, :, 1:row_count + 2] * wet_north[:, :, 2:row_count + 3])  16.3 us
    ppermute x12, starting transfers between devices, swapped(): lax.ppermute(shard, axis, [(i, i ^ 1 << distance) for i in range(lax.axis...  14.1 us
    slice x7, local copies, waits for them, and re-layouts, padded_2(): last = lax.slice_in_dim(shard, length - width, length, axis=dim)  13.2 us
    ppermute x12, waiting for transfers between devices, swapped(): lax.ppermute(shard, axis, [(i, i ^ 1 << distance) for i in range(lax.axis...  12.3 us
    concatenate x2, other arithmetic, padded_2(): shard = jnp.concatenate([before, shard, after], axis=dim)  12 us
  transfers between devices with their start and end apart: 24, of which 5 were waited for; matrix products, arithmetic and copies ran while one was open for 46% of the time, Pallas kernels for 0%

commit v1 on v0

v1 whole, which is shorter than its diff:
```python
import functools

import jax
import jax.numpy as jnp
from jax import lax
from jax.experimental import pallas as pl
from jax.experimental.pallas import tpu as pltpu
from jax.sharding import PartitionSpec as P

MESH = pl.DeviceIdType.MESH
SCALE = 0.2 / 6.0
PITCH = 20
CHUNKS = 4


def lanes():
    return lax.broadcasted_iota(jnp.int32, (8, 128), 1)


def spot():
    return lax.rem(lax.rem(lanes() + 4, 128), PITCH)


def roll(x, shift):
    shift = shift % 128 if isinstance(shift, int) else shift
    return x if isinstance(shift, int) and shift == 0 else pltpu.roll(x, shift, 1)


def ahead(pair):
    if len(pair) == 1:
        return [roll(pair[0], 127)]
    first, second = roll(pair[0], 127), roll(pair[1], 127)
    return [jnp.where(lanes() < 127, first, second), second]


def behind(pair):
    if len(pair) == 1:
        return [roll(pair[0], 1)]
    first, second = roll(pair[0], 1), roll(pair[1], 1)
    return [first, jnp.where(lanes() > 0, second, first)]


def each(function, *pairs):
    return [function(*items) for items in zip(*pairs)]


def tripled(pair):
    return each(lambda q: 3.0 * q, pair)


def face(weight, south, here, north, beyond):
    def one(w, a, b, c, d):
        return w * (2.0 * (b + c) + jnp.where(w > 0.0, 3.0 * b - a, 3.0 * c - d))

    return each(one, weight, south, here, north, beyond)


def east_change(weight, here):
    after = ahead(here)
    low = each(lambda q, r: 3.0 * q - r, here, behind(here))
    high = ahead(each(lambda q, r: 3.0 * q - r, here, after))
    flux = each(
        lambda w, q, r, l, h: w * (2.0 * (q + r) + jnp.where(w > 0.0, l, h)), weight, here, after, low, high
    )
    return each(lambda f, g: f - g, flux, behind(flux))


def updated(here, east, north, before, wet):
    return each(lambda q, e, n, m, s: (q - (e + (n - m))) * s, here, east, north, before, wet)


def north_fluxes(load, weight, offset):
    return [
        face(weight, load(k, offset - 1), load(k, offset), load(k, offset + 1), load(k, offset + 2)) for k in range(4)
    ]


def wet_faces(load, offset, along_rows):
    here = load(4, offset)
    other = load(4, offset + 1) if along_rows else ahead(here)
    return each(lambda a, b: a * b * SCALE, here, other)


def weights(load, faces, k, offset):
    return each(lambda w, s: w * s, load(k, offset), faces)


def local_position():
    return lax.axis_index("lon"), lax.axis_index("lat")


def advance_kernel(
    lon_count,
    lat_count,
    t_ref,
    s_ref,
    u_ref,
    v_ref,
    w_ref,
    out,
    strips_out,
    x0,
    x1,
    wet_int,
    east_wet,
    north_wet,
    rows_in,
    wet_rows_in,
    packed,
    packed_next,
    wires,
    wires_in,
    strip,
    strip_mid,
    strip_next,
    load_sem,
    row_send,
    row_recv,
    wire_send,
    wire_recv,
):
    inputs = (t_ref, s_ref, u_ref, v_ref, w_ref)
    layers, rows, _ = t_ref.shape
    stride = rows // 8
    north_pad = 8 + rows
    lon, lat = local_position()
    top = lat == lat_count - 1
    bottom = lat == 0
    east = {"lon": lax.rem(lon + 1, lon_count)}
    west = {"lon": lax.rem(lon + lon_count - 1, lon_count)}
    mirror = {"lon": lon_count - 1 - lon}

    loads = []
    for k in (4, 0, 1, 2, 3):
        for half in range(2):
            here = inputs[k].at[:, :, pl.ds(128 * half, 128)]
            there = wet_int.at[:, half] if k == 4 else x0.at[k, :, half, pl.ds(8, rows)]
            loads.append(pltpu.make_async_copy(here, there, load_sem.at[k, half]))
    for copy in loads:
        copy.start()

    barrier = pltpu.get_barrier_semaphore()
    pl.semaphore_signal(barrier, inc=1, device_id=east, device_id_type=MESH)
    pl.semaphore_signal(barrier, inc=1, device_id=west, device_id_type=MESH)

    @pl.when(top)
    def _():
        pl.semaphore_signal(barrier, inc=1, device_id=mirror, device_id_type=MESH)

    @pl.when(jnp.logical_not(top))
    def _():
        pl.semaphore_signal(barrier, inc=1, device_id={"lat": lat + 1}, device_id_type=MESH)

    @pl.when(jnp.logical_not(bottom))
    def _():
        pl.semaphore_signal(barrier, inc=1, device_id={"lat": lat - 1}, device_id_type=MESH)
        pl.semaphore_wait(barrier, 4)

    @pl.when(bottom)
    def _():
        pl.semaphore_wait(barrier, 3)

    def row_copies(first, there, side, device):
        copies = []
        for k in range(5):
            for half in range(2):
                source = inputs[k].at[:, pl.ds(first, 4), pl.ds(128 * half, 128)]
                if k == 4:
                    target = wet_rows_in.at[side, :, half, pl.ds(there, 4)]
                else:
                    target = rows_in.at[side, k, :, half, pl.ds(there, 4)]
                up = 0 if first else 1
                copies.append(
                    pltpu.make_async_remote_copy(
                        source,
                        target,
                        row_send.at[up, k, half],
                        row_recv.at[side, k, half],
                        device_id=device,
                        device_id_type=MESH,
                    )
                )
        return copies

    to_north = row_copies(rows - 4, 4, 0, {"lat": jnp.minimum(lat + 1, lat_count - 1)})
    to_mirror = row_copies(rows - 4, 4, 1, mirror)
    to_south = row_copies(0, 0, 1, {"lat": jnp.maximum(lat - 1, 0)})

    @pl.when(top)
    def _():
        for copy in to_mirror:
            copy.start()

    @pl.when(jnp.logical_not(top))
    def _():
        for copy in to_north:
            copy.start()

    @pl.when(jnp.logical_not(bottom))
    def _():
        for copy in to_south:
            copy.start()

    for copy in loads:
        copy.wait()

    def pack(source):
        place = lax.rem(lanes() + 4, 128)
        total = None
        for layer in reversed(range(layers)):
            both = jnp.where(lanes() < 64, source(layer, 0), source(layer, 1))
            moved = roll(both, PITCH * layer)
            if total is None:
                total = moved
            else:
                total = jnp.where(place < PITCH * (layer + 1) - 6, moved, total)
        return jnp.where(place < 120, total, moved)

    def pack_tile(row):
        tile = pl.ds(pl.multiple_of(row, 8), 8)
        group = spot() // 4
        group_west = lax.rem(lanes(), PITCH) // 4
        east_wire = west_wire = None
        for k in range(5):
            one = pack(lambda layer, half: x0[k, layer, half, tile, :])
            packed[k, tile, :] = one
            moved = roll(one, 4 * k)
            east_wire = moved if k == 0 else jnp.where(group == k, moved, east_wire)
            west_wire = moved if k == 0 else jnp.where(group_west == k, moved, west_wire)
        wires[0, tile, :] = east_wire
        wires[1, tile, :] = west_wire

    def wire_copies(start, count, number):
        return [
            pltpu.make_async_remote_copy(
                wires.at[side, pl.ds(start, count)],
                wires_in.at[side, pl.ds(start, count)],
                wire_send.at[side, number],
                wire_recv.at[side, number],
                device_id=device,
                device_id_type=MESH,
            )
            for side, device in ((0, east), (1, west))
        ]

    wire_parts = []
    tiles = rows // 8
    for chunk in range(CHUNKS):
        low, high = tiles * chunk // CHUNKS, tiles * (chunk + 1) // CHUNKS

        @pl.loop(low, high)
        def _(i):
            row = pl.multiple_of(8 + 8 * i, 8)

            @pl.loop(0, layers)
            def _(layer):
                for half in range(2):
                    part = wet_int[layer, half, pl.ds(pl.multiple_of(8 * i, 8), 8), :]
                    x0[4, layer, half, pl.ds(row, 8), :] = part.astype(jnp.float32)

            pack_tile(row)

        copies = wire_copies(8 + 8 * low, 8 * (high - low), chunk)
        for copy in copies:
            copy.start()
        wire_parts += copies

    def whole_blocks(source, target, first_step):
        @pl.loop(0, layers)
        def _(layer):
            def wet_at(offset):
                return [x0[4, layer, half, pl.ds(offset, 8, stride=stride), :] for half in range(2)]

            def loader(t):
                def load(k, offset):
                    at = pl.ds(8 + t + offset, 8, stride=stride)
                    return [(x0 if k == 4 else source)[k, layer, half, at, :] for half in range(2)]

                return load

            def faces(load, t, offset, along_rows):
                kept = north_wet if along_rows else east_wet
                at = pl.ds(8 + t + offset, 8, stride=stride)
                if not first_step:
                    return [kept[layer, half, at, :] for half in range(2)]
                made = wet_faces(load, offset, along_rows)
                if offset == 0:
                    for half in range(2):
                        kept[layer, half, at, :] = made[half]
                return made

            start = loader(0)
            before = north_fluxes(start, weights(start, faces(start, 0, -1, True), 3, -1), -1)

            def body(t, before):
                load = loader(t)
                north = north_fluxes(load, weights(load, faces(load, t, 0, True), 3, 0), 0)
                across = weights(load, faces(load, t, 0, False), 2, 0)
                wet = wet_at(8 + t)
                for k in range(4):
                    here = load(k, 0)
                    new = updated(here, east_change(across, here), north[k], before[k], wet)
                    for half in range(2):
                        target[k, layer, half, pl.ds(8 + t, 8, stride=stride), :] = new[half]
                return north

            lax.fori_loop(0, stride, body, before)

    sublane = lax.broadcasted_iota(jnp.int32, (8, 128), 0)

    def eight_rows(source, layer, first):
        def load(k, offset):
            at = pl.ds(first + offset, 8)
            return [(x0 if k == 4 else source)[k, layer, half, at, :] for half in range(2)]

        return load

    def changed_rows(load, across_wet, north_here, north_before, folded):
        late = 1 if folded else 0
        north = north_fluxes(load, weights(load, north_here, 3, late), 0)
        before = north_fluxes(load, weights(load, north_before, 3, late - 1), -1)
        speed = ahead(load(2, 0)) if folded else load(2, 0)
        across = each(lambda w, s: w * s, speed, across_wet)
        wet = load(4, 0)
        return [
            updated(load(k, 0), east_change(across, load(k, 0)), north[k], before[k], wet) for k in range(4)
        ]

    def edge_rows(source, target, starts, first_step):
        right = jnp.logical_and(sublane >= 2, sublane < 6)

        @pl.loop(0, layers)
        def _(layer):
            for first in starts:
                load = eight_rows(source, layer, first)
                at = pl.ds(first, 8)
                if first_step:
                    across_wet = wet_faces(load, 0, False)
                    north_here = wet_faces(load, 0, True)
                    north_before = wet_faces(load, -1, True)
                    for half in range(2):
                        east_wet[layer, half, at, :] = across_wet[half]
                        north_wet[layer, half, at, :] = north_here[half]
                else:
                    across_wet = [east_wet[layer, half, at, :] for half in range(2)]
                    north_here = [north_wet[layer, half, at, :] for half in range(2)]
                    north_before = [north_wet[layer, half, pl.ds(first - 1, 8), :] for half in range(2)]
                new = changed_rows(load, across_wet, north_here, north_before, False)
                for k in range(4):
                    for half in range(2):
                        old = target[k, layer, half, at, :]
                        target[k, layer, half, at, :] = jnp.where(right, new[k][half], old)

    past_fold = jnp.logical_and(sublane >= 4, sublane < 6)

    def fold_rows():
        first = north_pad - 4
        at = pl.ds(first, 8)

        @pl.loop(0, layers)
        def _(layer):
            load = eight_rows(x0, layer, first)
            made = [wet_faces(load, 0, False), wet_faces(load, 0, True), wet_faces(load, -1, True)]
            new = changed_rows(load, *made, True)
            for k in range(4):
                for half in range(2):
                    x1[k, layer, half, at, :] = jnp.where(past_fold, new[k][half], x1[k, layer, half, at, :])

    whole_blocks(x0, x1, True)

    @pl.when(bottom)
    def _():
        @pl.loop(0, layers)
        def _(layer):
            for half in range(2):
                for k in range(5):
                    x0[k, layer, half, pl.ds(0, 8), :] = jnp.zeros((8, 128), jnp.float32)

    @pl.when(jnp.logical_not(bottom))
    def _():
        for copy in row_copies(0, 4, 0, east):
            copy.wait_recv()

        @pl.loop(0, layers)
        def _(layer):
            for half in range(2):
                for k in range(4):
                    x0[k, layer, half, pl.ds(0, 8), :] = rows_in[0, k, layer, half]
                x0[4, layer, half, pl.ds(0, 8), :] = wet_rows_in[0, layer, half].astype(jnp.float32)

    for copy in to_south:
        copy.wait_recv()

    def north_tile(k, layer, half):
        return wet_rows_in[1, layer, half].astype(jnp.float32) if k == 4 else rows_in[1, k, layer, half]

    @pl.when(jnp.logical_not(top))
    def _():
        @pl.loop(0, layers)
        def _(layer):
            for half in range(2):
                for k in range(5):
                    x0[k, layer, half, pl.ds(north_pad, 8), :] = north_tile(k, layer, half)

    @pl.when(top)
    def _():
        @pl.loop(0, layers)
        def _(layer):
            for half in range(2):
                for k in range(5):
                    flipped = jnp.take_along_axis(north_tile(k, layer, 1 - half), 127 - lanes(), axis=1)
                    if k in (2, 3):
                        flipped = -flipped
                    for row in range(4):
                        x0[k, layer, half, pl.ds(north_pad + row, 1), :] = flipped[7 - row : 8 - row, :]

    pack_tile(0)
    pack_tile(north_pad)
    for number, start in ((CHUNKS, 0), (CHUNKS + 1, north_pad)):
        copies = wire_copies(start, 8, number)
        for copy in copies:
            copy.start()
        wire_parts += copies

    edge_rows(x0, x1, (4, north_pad - 4), True)
    pl.when(top)(fold_rows)
    whole_blocks(x1, out, False)
    edge_rows(x1, out, (6, north_pad - 6), False)

    @pl.loop(0, tiles + 2)
    def _(i):
        tile = pl.ds(pl.multiple_of(8 * i, 8), 8)
        for k in range(5):
            source = x0 if k == 4 else x1
            packed_next[k, tile, :] = pack(lambda layer, half: source[k, layer, half, tile, :])

    for copy in wire_parts:
        copy.wait_recv()

    @pl.loop(0, tiles + 2)
    def _(i):
        tile = pl.ds(pl.multiple_of(8 * i, 8), 8)
        place = spot()
        for k in range(5):
            own = packed[k, tile, :]
            left = jnp.where(place < 4, roll(wires_in[0, tile, :], -4 * k), own)
            right = jnp.where(place < 4, own, roll(wires_in[1, tile, :], -4 * k))
            strip[k, tile, :] = jnp.where(place < 8, left, roll(right, 8))

    def strip_step(source, start, count, put):
        def loader(t):
            def load(k, offset):
                return [source[k, pl.ds(start + t + offset, 8, stride=stride), :]]

            return load

        first = loader(0)
        before = north_fluxes(first, weights(first, wet_faces(first, -1, True), 3, -1), -1)

        def body(t, before):
            load = loader(t)
            north = north_fluxes(load, weights(load, wet_faces(load, 0, True), 3, 0), 0)
            across = weights(load, wet_faces(load, 0, False), 2, 0)
            wet = load(4, 0)
            for k in range(4):
                here = load(k, 0)
                put(k, t, updated(here, east_change(across, here), north[k], before[k], wet)[0])
            return north

        lax.fori_loop(0, count, body, before)

    def put_mid(k, t, value):
        strip_mid[k, pl.ds(6 + t, 8, stride=stride), :] = value

    strip_step(strip, 6, stride + 4, put_mid)

    @pl.when(top)
    def _():
        first = north_pad - 4

        def load(k, offset):
            return [strip[k, pl.ds(first + offset, 8), :]]

        made = [wet_faces(load, 0, False), wet_faces(load, 0, True), wet_faces(load, -1, True)]
        new = changed_rows(load, *made, True)
        for k in range(4):
            at = pl.ds(first, 8)
            strip_mid[k, at, :] = jnp.where(past_fold, new[k][0], strip_mid[k, at, :])

    @pl.loop(0, tiles + 2)
    def _(i):
        tile = pl.ds(pl.multiple_of(8 * i, 8), 8)
        place = spot()
        for k in range(5):
            outer = strip[4, tile, :] if k == 4 else strip_mid[k, tile, :]
            inner = packed_next[k, tile, :]
            left = jnp.where(place < 4, roll(outer, -2), roll(inner, -2))
            right = jnp.where(place < 12, roll(inner, 10), roll(outer, 2))
            strip_next[k, tile, :] = jnp.where(place < 8, left, right)

    def put_out(k, t, value):
        place = spot()
        inside = jnp.logical_and(place >= 2, place < 6)
        strips_out[k, pl.ds(t, 8, stride=stride), :] = jnp.where(inside, value, roll(value, -12))

    strip_step(strip_next, 8, stride, put_out)

    for copy in wire_parts:
        copy.wait_send()
    for copy in to_mirror:
        copy.wait_send()

    @pl.when(jnp.logical_not(bottom))
    def _():
        for copy in to_south:
            copy.wait_send()


def write_kernel(blocks, strips, t_out, s_out, u_out, v_out, whole, sem):
    layers, rows, _ = t_out.shape
    copies = []
    for k, output in enumerate((t_out, s_out, u_out, v_out)):
        for layer in range(layers):

            @pl.loop(0, rows // 8)
            def _(i):
                start = pl.multiple_of(8 * i, 8)
                moved = roll(strips[k, pl.ds(start, 8), :], (2 - PITCH * layer) % 128)
                for half in range(2):
                    edge = lanes() < 4 if half == 0 else lanes() >= 124
                    block = blocks[k, layer, half, pl.ds(start + 8, 8), :]
                    whole[k, layer, half, pl.ds(start, 8), :] = jnp.where(edge, moved, block)

            for half in range(2):
                there = output.at[layer, :, pl.ds(128 * half, 128)]
                copy = pltpu.make_async_copy(whole.at[k, layer, half], there, sem.at[k, layer, half])
                copy.start()
                copies.append(copy)
    for copy in copies:
        copy.wait()


def local(lon_count, lat_count, *arrays):
    layers, rows, columns = arrays[0].shape
    padded = rows + 16
    vmem = pl.BlockSpec(memory_space=pltpu.VMEM)
    anywhere = pl.BlockSpec(memory_space=pltpu.HBM)
    dma = pltpu.SemaphoreType.DMA
    f32 = jnp.float32
    blocks, strips = pl.pallas_call(
        functools.partial(advance_kernel, lon_count, lat_count),
        name="advance",
        out_shape=(
            jax.ShapeDtypeStruct((4, layers, 2, padded, 128), f32),
            jax.ShapeDtypeStruct((4, rows, 128), f32),
        ),
        in_specs=[anywhere] * 5,
        out_specs=(vmem, vmem),
        scratch_shapes=[
            pltpu.VMEM((5, layers, 2, padded, 128), f32),
            pltpu.VMEM((4, layers, 2, padded, 128), f32),
            pltpu.VMEM((layers, 2, rows, 128), jnp.int32),
            pltpu.VMEM((layers, 2, padded, 128), f32),
            pltpu.VMEM((layers, 2, padded, 128), f32),
            pltpu.VMEM((2, 4, layers, 2, 8, 128), f32),
            pltpu.VMEM((2, layers, 2, 8, 128), jnp.int32),
            pltpu.VMEM((5, padded, 128), f32),
            pltpu.VMEM((5, padded, 128), f32),
            pltpu.VMEM((2, padded, 128), f32),
            pltpu.VMEM((2, padded, 128), f32),
            pltpu.VMEM((5, padded, 128), f32),
            pltpu.VMEM((4, padded, 128), f32),
            pltpu.VMEM((5, padded, 128), f32),
            dma((5, 2)),
            dma((2, 5, 2)),
            dma((2, 5, 2)),
            dma((2, CHUNKS + 2)),
            dma((2, CHUNKS + 2)),
        ],
        compiler_params=pltpu.CompilerParams(collective_id=0, has_side_effects=True, vmem_limit_bytes=40 << 20),
    )(*(pltpu.with_memory_space_constraint(array, pltpu.HBM) for array in arrays))
    return pl.pallas_call(
        write_kernel,
        name="write",
        out_shape=tuple(jax.ShapeDtypeStruct((layers, rows, columns), f32) for _ in range(4)),
        in_specs=[vmem, vmem],
        out_specs=(anywhere,) * 4,
        scratch_shapes=[pltpu.VMEM((4, layers, 2, rows, 128), f32), dma((4, layers, 2))],
        compiler_params=pltpu.CompilerParams(vmem_limit_bytes=40 << 20),
    )(blocks, strips)


def solution(mesh):
    placed = P(None, "lat", "lon")
    return jax.shard_map(
        functools.partial(local, mesh.shape["lon"], mesh.shape["lat"]),
        mesh=mesh,
        in_specs=(placed,) * 5,
        out_specs=(placed,) * 4,
        check_vma=False,
    )
```

time: 195 us -> 146 us (0.75)
  the two profiles are of different devices: /device:TPU:25 before, /device:TPU:27 now
where the time goes in v1:
time: 146 us
  Pallas kernels  145 us (99%)
    pallas_call x1, Pallas kernels, local(): pl.pallas_call(functools.partial(advance_kernel, lon_count, lat_count), n...  104 us
    pallas_call x1, Pallas kernels, local(): pl.pallas_call(write_kernel, name='write', out_shape=tuple((jax.ShapeDtyp...  40.9 us

profile of v1, /device:TPU:27, one launch (start us, length us, event | category | flops | bytes accessed | tf_op | source)
XLA Modules:
  0.0 146.0 jit_solution(5634807706891758605)
XLA Ops:
  0.6 104.4 %advance.1 = (f32[4,6,2,208,128]{4,3,2,1,0:T(8,128)S(1)}, f32[4,192,128]{2,1,0:T(8,128)S(1)}) custom-call(f32[6,192,256]{2,1,0:T(8,128)} %t_ref.1, f32[6,192,256]{2,1,0:T(8,128)} %s_ref.1, f32[6,192,256]{2,1,0:T(8,128)} %u_ref.1, f32[6,192,256]{2,1,0:T(8,128)} %v_ref.1, s32[6,192,256]{2,1,0:T(8,128)} %w_ref.1), custom_call_target="tpu_custom_call" | custom-call | tf_op jit(solution)/shard_map/advance/pallas_call | solution.py:550
  105.1 40.9 %write.1 = (f32[6,192,256]{2,1,0:T(8,128)}, f32[6,192,256]{2,1,0:T(8,128)}, f32[6,192,256]{2,1,0:T(8,128)}, f32[6,192,256]{2,1,0:T(8,128)}) custom-call(f32[4,6,2,208,128]{4,3,2,1,0:T(8,128)S(1)} %get-tuple-element.6.blocks, f32[4,192,128]{2,1,0:T(8,128)S(1)} %get-tuple-element.7.strips), custom_call_target="tpu_custom_call" | custom-call | tf_op jit(solution)/shard_map/write/pallas_call | solution.py:582

commit v2 on v1

v2 whole, which is shorter than its diff:
```python
import functools

import jax
import jax.numpy as jnp
from jax import lax
from jax.experimental import pallas as pl
from jax.experimental.pallas import tpu as pltpu
from jax.sharding import PartitionSpec as P

MESH = pl.DeviceIdType.MESH
SCALE = 0.2 / 6.0
PITCH = 20
CHUNKS = 4
WRITTEN = 6
PACKED = 2
EDGES = 3
BLOCKS = 6
STRIPS = 5


def lanes():
    return lax.broadcasted_iota(jnp.int32, (8, 128), 1)


def spot():
    return lax.rem(lax.rem(lanes() + 4, 128), PITCH)


def roll(x, shift):
    shift = shift % 128 if isinstance(shift, int) else shift
    return x if isinstance(shift, int) and shift == 0 else pltpu.roll(x, shift, 1)


def shifted(values, distance):
    moved = [roll(value, -distance) for value in values]
    if len(moved) == 1:
        return moved
    first, second = moved
    if distance > 0:
        return [jnp.where(lanes() < 128 - distance, first, second), second]
    return [first, jnp.where(lanes() >= -distance, second, first)]


def face(weight, positive, before, here, after, beyond):
    return weight * (2.0 * (here + after) + jnp.where(positive, 3.0 * here - before, 3.0 * after - beyond))


def fluxes(weight, fields):
    positive = [w > 0.0 for w in weight]
    return [[face(*values) for values in zip(weight, positive, *field)] for field in fields]


def tiles_step(tiles):
    across = []
    for load, _, _, _, _ in tiles:
        here = [load(k, 0) for k in range(4)]
        across.append([(shifted(q, -1), q, shifted(q, 1), shifted(q, 2)) for q in here])
    weights = []
    for (load, faces, _, _, late), fields in zip(tiles, across):
        east_wet, north_wet = faces()
        u = fields[2][2] if late else fields[2][1]
        v = load(3, 1) if late else fields[3][1]
        weights.append(([q * s for q, s in zip(u, east_wet)], [q * s for q, s in zip(v, north_wet)]))
    east = []
    for fields, (weight, _) in zip(across, weights):
        flux = fluxes(weight, fields)
        east.append([(f, shifted(f, -1)) for f in flux])
    for (load, _, south, put, _), fields, (_, weight), changes in zip(tiles, across, weights, east):
        wet = load(4, 0)
        north = fluxes(weight, [(load(k, -1), fields[k][1], load(k, 1), load(k, 2)) for k in range(4)])
        for k in range(4):
            flux, west = changes[k]
            parts = zip(fields[k][1], flux, west, north[k], south(k, north[k]), wet)
            put(k, [(q - ((e - w) + (n - m))) * s for q, e, w, n, m, s in parts])


def rolled_south(k, flux):
    return [pltpu.roll(value, 1, 0) for value in flux]


def wet_faces(load):
    here = load(4, 0)
    pairs = zip(here, shifted(here, 1), load(4, 1))
    made = [(w * e * SCALE, w * n * SCALE) for w, e, n in pairs]
    return [m[0] for m in made], [m[1] for m in made]


def local_position():
    return lax.axis_index("lon"), lax.axis_index("lat")


def advance_kernel(
    lon_count,
    lat_count,
    t_ref,
    s_ref,
    u_ref,
    v_ref,
    w_ref,
    out,
    strips_out,
    x0,
    x1,
    wet_int,
    east_wet,
    north_wet,
    rows_in,
    wet_rows_in,
    packed,
    packed_next,
    wires,
    wires_in,
    strip,
    strip_mid,
    strip_next,
    flows,
    strip_flows,
    load_sem,
    row_send,
    row_recv,
    wire_send,
    wire_recv,
):
    inputs = (t_ref, s_ref, u_ref, v_ref, w_ref)
    layers, rows, _ = t_ref.shape
    north_pad = 8 + rows
    lon, lat = local_position()
    top = lat == lat_count - 1
    bottom = lat == 0
    east = {"lon": lax.rem(lon + 1, lon_count)}
    west = {"lon": lax.rem(lon + lon_count - 1, lon_count)}
    mirror = {"lon": lon_count - 1 - lon}

    loads = []
    for k in (4, 0, 1, 2, 3):
        for half in range(2):
            here = inputs[k].at[:, :, pl.ds(128 * half, 128)]
            there = wet_int.at[:, half] if k == 4 else x0.at[k, :, half, pl.ds(8, rows)]
            loads.append(pltpu.make_async_copy(here, there, load_sem.at[k, half]))
    for copy in loads:
        copy.start()

    barrier = pltpu.get_barrier_semaphore()
    pl.semaphore_signal(barrier, inc=1, device_id=east, device_id_type=MESH)
    pl.semaphore_signal(barrier, inc=1, device_id=west, device_id_type=MESH)

    @pl.when(top)
    def _():
        pl.semaphore_signal(barrier, inc=1, device_id=mirror, device_id_type=MESH)

    @pl.when(jnp.logical_not(top))
    def _():
        pl.semaphore_signal(barrier, inc=1, device_id={"lat": lat + 1}, device_id_type=MESH)

    @pl.when(jnp.logical_not(bottom))
    def _():
        pl.semaphore_signal(barrier, inc=1, device_id={"lat": lat - 1}, device_id_type=MESH)
        pl.semaphore_wait(barrier, 4)

    @pl.when(bottom)
    def _():
        pl.semaphore_wait(barrier, 3)

    def row_copies(first, there, side, device):
        copies = []
        for k in range(5):
            for half in range(2):
                source = inputs[k].at[:, pl.ds(first, 4), pl.ds(128 * half, 128)]
                if k == 4:
                    target = wet_rows_in.at[side, :, half, pl.ds(there, 4)]
                else:
                    target = rows_in.at[side, k, :, half, pl.ds(there, 4)]
                up = 0 if first else 1
                copies.append(
                    pltpu.make_async_remote_copy(
                        source,
                        target,
                        row_send.at[up, k, half],
                        row_recv.at[side, k, half],
                        device_id=device,
                        device_id_type=MESH,
                    )
                )
        return copies

    to_north = row_copies(rows - 4, 4, 0, {"lat": jnp.minimum(lat + 1, lat_count - 1)})
    to_mirror = row_copies(rows - 4, 4, 1, mirror)
    to_south = row_copies(0, 0, 1, {"lat": jnp.maximum(lat - 1, 0)})

    @pl.when(top)
    def _():
        for copy in to_mirror:
            copy.start()

    @pl.when(jnp.logical_not(top))
    def _():
        for copy in to_north:
            copy.start()

    @pl.when(jnp.logical_not(bottom))
    def _():
        for copy in to_south:
            copy.start()

    for copy in loads:
        copy.wait()

    def pack(source):
        place = lax.rem(lanes() + 4, 128)
        total = None
        for layer in reversed(range(layers)):
            both = jnp.where(lanes() < 64, source(layer, 0), source(layer, 1))
            moved = roll(both, PITCH * layer)
            if total is None:
                total = moved
            else:
                total = jnp.where(place < PITCH * (layer + 1) - 6, moved, total)
        return jnp.where(place < 120, total, moved)

    def pack_tiles(starts):
        group = spot() // 4
        group_west = lax.rem(lanes(), PITCH) // 4
        own = []
        for row in starts:
            tile = pl.ds(row, 8)
            own.append([pack(lambda layer, half: x0[k, layer, half, tile, :]) for k in range(5)])
        moved = [[roll(one, 4 * k) for k, one in enumerate(ones)] for ones in own]
        for row, ones, others in zip(starts, own, moved):
            tile = pl.ds(row, 8)
            east_wire, west_wire = others[0], others[0]
            for k in range(5):
                packed[k, tile, :] = ones[k]
                east_wire = jnp.where(group == k, others[k], east_wire)
                west_wire = jnp.where(group_west == k, others[k], west_wire)
            wires[0, tile, :] = east_wire
            wires[1, tile, :] = west_wire

    def wire_copies(start, count, number):
        return [
            pltpu.make_async_remote_copy(
                wires.at[side, pl.ds(start, count)],
                wires_in.at[side, pl.ds(start, count)],
                wire_send.at[side, number],
                wire_recv.at[side, number],
                device_id=device,
                device_id_type=MESH,
            )
            for side, device in ((0, east), (1, west))
        ]

    wire_parts = []
    tiles = rows // 8
    for chunk in range(CHUNKS):
        low, high = tiles * chunk // CHUNKS, tiles * (chunk + 1) // CHUNKS

        @pl.loop(0, (high - low) // PACKED)
        def _(i):
            first = pl.multiple_of(8 * (low + PACKED * i), 8)
            for layer in range(layers):
                for half in range(2):
                    part = wet_int[layer, half, pl.ds(first, 8 * PACKED), :]
                    x0[4, layer, half, pl.ds(first + 8, 8 * PACKED), :] = part.astype(jnp.float32)
            pack_tiles([pl.multiple_of(first + 8 + 8 * j, 8) for j in range(PACKED)])

        copies = wire_copies(8 + 8 * low, 8 * (high - low), chunk)
        for copy in copies:
            copy.start()
        wire_parts += copies

    def loader(source, layer, first):
        def load(k, offset):
            at = pl.ds(first + offset, 8)
            return [(x0 if k == 4 else source)[k, layer, half, at, :] for half in range(2)]

        return load

    def face_weights(load, layer, first, first_step):
        def faces():
            at = pl.ds(first, 8)
            if not first_step:
                return tuple([kept[layer, half, at, :] for half in range(2)] for kept in (east_wet, north_wet))
            made = wet_faces(load)
            for kept, parts in zip((east_wet, north_wet), made):
                for half in range(2):
                    kept[layer, half, at, :] = parts[half]
            return made

        return faces

    def whole_blocks(source, target, first_step):
        def tile(layer, first):
            at = pl.ds(first, 8)

            def south(k, flux):
                for half in range(2):
                    flows[k, half, at, :] = flux[half]
                return [flows[k, half, pl.ds(first - 1, 8), :] for half in range(2)]

            def put(k, new):
                for half in range(2):
                    target[k, layer, half, at, :] = new[half]

            load = loader(source, layer, first)
            return load, face_weights(load, layer, first, first_step), south, put, False

        @pl.loop(0, layers)
        def _(layer):
            @pl.loop(0, rows // (8 * BLOCKS))
            def _(i):
                first = pl.multiple_of(8 + 8 * BLOCKS * i, 8)
                tiles_step([tile(layer, first + 8 * j) for j in range(BLOCKS)])

    sublane = lax.broadcasted_iota(jnp.int32, (8, 128), 0)

    def edge_rows(source, target, first, first_step):
        right = jnp.logical_and(sublane >= 2, sublane < 6)

        def tile(layer):
            at = pl.ds(first, 8)

            def put(k, new):
                for half in range(2):
                    target[k, layer, half, at, :] = jnp.where(right, new[half], target[k, layer, half, at, :])

            load = loader(source, layer, first)
            return load, face_weights(load, layer, first, first_step), rolled_south, put, False

        @pl.loop(0, layers // EDGES)
        def _(i):
            tiles_step([tile(EDGES * i + j) for j in range(EDGES)])

    past_fold = jnp.logical_and(sublane >= 4, sublane < 6)

    def fold_rows():
        first = north_pad - 4

        def tile(layer):
            at = pl.ds(first, 8)

            def put(k, new):
                for half in range(2):
                    x1[k, layer, half, at, :] = jnp.where(past_fold, new[half], x1[k, layer, half, at, :])

            load = loader(x0, layer, first)
            return load, lambda: wet_faces(load), rolled_south, put, True

        @pl.loop(0, layers // EDGES)
        def _(i):
            tiles_step([tile(EDGES * i + j) for j in range(EDGES)])

    whole_blocks(x0, x1, True)

    @pl.when(bottom)
    def _():
        @pl.loop(0, layers)
        def _(layer):
            for half in range(2):
                for k in range(5):
                    x0[k, layer, half, pl.ds(0, 8), :] = jnp.zeros((8, 128), jnp.float32)

    @pl.when(jnp.logical_not(bottom))
    def _():
        for copy in row_copies(0, 4, 0, east):
            copy.wait_recv()

        @pl.loop(0, layers)
        def _(layer):
            for half in range(2):
                for k in range(4):
                    x0[k, layer, half, pl.ds(0, 8), :] = rows_in[0, k, layer, half]
                x0[4, layer, half, pl.ds(0, 8), :] = wet_rows_in[0, layer, half].astype(jnp.float32)

    for copy in to_south:
        copy.wait_recv()

    def north_tile(k, layer, half):
        return wet_rows_in[1, layer, half].astype(jnp.float32) if k == 4 else rows_in[1, k, layer, half]

    @pl.when(jnp.logical_not(top))
    def _():
        @pl.loop(0, layers)
        def _(layer):
            for half in range(2):
                for k in range(5):
                    x0[k, layer, half, pl.ds(north_pad, 8), :] = north_tile(k, layer, half)

    @pl.when(top)
    def _():
        @pl.loop(0, layers)
        def _(layer):
            for half in range(2):
                for k in range(5):
                    flipped = jnp.take_along_axis(north_tile(k, layer, 1 - half), 127 - lanes(), axis=1)
                    if k in (2, 3):
                        flipped = -flipped
                    for row in range(4):
                        x0[k, layer, half, pl.ds(north_pad + row, 1), :] = flipped[7 - row : 8 - row, :]

    pack_tiles([0, north_pad])
    for number, start in ((CHUNKS, 0), (CHUNKS + 1, north_pad)):
        copies = wire_copies(start, 8, number)
        for copy in copies:
            copy.start()
        wire_parts += copies

    edge_rows(x0, x1, 4, True)
    edge_rows(x0, x1, north_pad - 4, True)
    pl.when(top)(fold_rows)
    whole_blocks(x1, out, False)
    edge_rows(x1, out, 6, False)
    edge_rows(x1, out, north_pad - 6, False)

    def every_tile(function):
        @pl.loop(0, (tiles + 2) // 2)
        def _(i):
            function([pl.ds(pl.multiple_of(16 * i + 8 * j, 8), 8) for j in range(2)])

    def pack_next(at):
        for tile in at:
            for k in range(5):
                source = x0 if k == 4 else x1
                packed_next[k, tile, :] = pack(lambda layer, half: source[k, layer, half, tile, :])

    every_tile(pack_next)

    for copy in wire_parts:
        copy.wait_recv()

    def join(at):
        place = spot()
        parts = []
        for tile in at:
            from_west, from_east = wires_in[0, tile, :], wires_in[1, tile, :]
            for k in range(5):
                own = packed[k, tile, :]
                parts.append((tile, k, roll(from_west, -4 * k), own, roll(own, 8), roll(from_east, 8 - 4 * k)))
        for tile, k, west_halo, west_edge, east_edge, east_halo in parts:
            left = jnp.where(place < 4, west_halo, west_edge)
            right = jnp.where(place < 12, east_edge, east_halo)
            strip[k, tile, :] = jnp.where(place < 8, left, right)

    every_tile(join)

    def strip_tile(source, first, put, south=None, late=False):
        def load(k, offset):
            return [source[k, pl.ds(first + offset, 8), :]]

        def stored(k, flux):
            strip_flows[k, pl.ds(first, 8), :] = flux[0]
            return [strip_flows[k, pl.ds(first - 1, 8), :]]

        return load, lambda: wet_faces(load), south or stored, functools.partial(put, first), late

    def strip_step(source, put):
        @pl.loop(0, (tiles + 1) // STRIPS)
        def _(i):
            first = 4 + 8 * STRIPS * i
            tiles_step([strip_tile(source, first + 8 * j, put) for j in range(STRIPS)])

    def put_mid(first, k, new):
        strip_mid[k, pl.ds(first, 8), :] = new[0]

    strip_step(strip, put_mid)

    @pl.when(top)
    def _():
        def put(first, k, new):
            at = pl.ds(first, 8)
            strip_mid[k, at, :] = jnp.where(past_fold, new[0], strip_mid[k, at, :])

        tiles_step([strip_tile(strip, north_pad - 4, put, rolled_south, True)])

    def join_next(at):
        place = spot()
        parts = []
        for tile in at:
            for k in range(5):
                outer = strip[4, tile, :] if k == 4 else strip_mid[k, tile, :]
                inner = packed_next[k, tile, :]
                parts.append((tile, k, roll(outer, -2), roll(inner, -2), roll(inner, 10), roll(outer, 2)))
        for tile, k, west_outer, west_inner, east_inner, east_outer in parts:
            left = jnp.where(place < 4, west_outer, west_inner)
            right = jnp.where(place < 12, east_inner, east_outer)
            strip_next[k, tile, :] = jnp.where(place < 8, left, right)

    every_tile(join_next)

    def put_out(first, k, new):
        place = spot()
        inside = jnp.logical_and(place >= 2, place < 6)
        strips_out[k, pl.ds(first, 8), :] = jnp.where(inside, new[0], roll(new[0], -12))

    strip_step(strip_next, put_out)

    for copy in wire_parts:
        copy.wait_send()
    for copy in to_mirror:
        copy.wait_send()

    @pl.when(jnp.logical_not(bottom))
    def _():
        for copy in to_south:
            copy.wait_send()


def write_kernel(blocks, strips, t_out, s_out, u_out, v_out, whole, sem):
    layers, rows, _ = t_out.shape
    copies = []
    for k, output in enumerate((t_out, s_out, u_out, v_out)):

        @pl.loop(0, rows // (8 * WRITTEN))
        def _(i):
            first = pl.multiple_of(8 * WRITTEN * i, 8)
            starts = [pl.multiple_of(first + 8 * j, 8) for j in range(WRITTEN)]
            strip = [strips[k, pl.ds(start + 8, 8), :] for start in starts]
            moved = [[roll(value, 2 - PITCH * layer) for layer in range(layers)] for value in strip]
            for start, values in zip(starts, moved):
                for layer in range(layers):
                    for half in range(2):
                        edge = lanes() < 4 if half == 0 else lanes() >= 124
                        block = blocks[k, layer, half, pl.ds(start + 8, 8), :]
                        whole[k, layer, half, pl.ds(start, 8), :] = jnp.where(edge, values[layer], block)

        for layer in range(layers):
            for half in range(2):
                there = output.at[layer, :, pl.ds(128 * half, 128)]
                copy = pltpu.make_async_copy(whole.at[k, layer, half], there, sem.at[k, layer, half])
                copy.start()
                copies.append(copy)
    for copy in copies:
        copy.wait()


def local(lon_count, lat_count, *arrays):
    layers, rows, columns = arrays[0].shape
    padded = rows + 16
    vmem = pl.BlockSpec(memory_space=pltpu.VMEM)
    anywhere = pl.BlockSpec(memory_space=pltpu.HBM)
    dma = pltpu.SemaphoreType.DMA
    f32 = jnp.float32
    blocks, strips = pl.pallas_call(
        functools.partial(advance_kernel, lon_count, lat_count),
        name="advance",
        out_shape=(
            jax.ShapeDtypeStruct((4, layers, 2, padded, 128), f32),
            jax.ShapeDtypeStruct((4, padded, 128), f32),
        ),
        in_specs=[anywhere] * 5,
        out_specs=(vmem, vmem),
        scratch_shapes=[
            pltpu.VMEM((5, layers, 2, padded, 128), f32),
            pltpu.VMEM((4, layers, 2, padded, 128), f32),
            pltpu.VMEM((layers, 2, rows, 128), jnp.int32),
            pltpu.VMEM((layers, 2, padded, 128), f32),
            pltpu.VMEM((layers, 2, padded, 128), f32),
            pltpu.VMEM((2, 4, layers, 2, 8, 128), f32),
            pltpu.VMEM((2, layers, 2, 8, 128), jnp.int32),
            pltpu.VMEM((5, padded, 128), f32),
            pltpu.VMEM((5, padded, 128), f32),
            pltpu.VMEM((2, padded, 128), f32),
            pltpu.VMEM((2, padded, 128), f32),
            pltpu.VMEM((5, padded, 128), f32),
            pltpu.VMEM((4, padded, 128), f32),
            pltpu.VMEM((5, padded, 128), f32),
            pltpu.VMEM((4, 2, padded, 128), f32),
            pltpu.VMEM((4, padded, 128), f32),
            dma((5, 2)),
            dma((2, 5, 2)),
            dma((2, 5, 2)),
            dma((2, CHUNKS + 2)),
            dma((2, CHUNKS + 2)),
        ],
        compiler_params=pltpu.CompilerParams(collective_id=0, has_side_effects=True, vmem_limit_bytes=40 << 20),
    )(*(pltpu.with_memory_space_constraint(array, pltpu.HBM) for array in arrays))
    return pl.pallas_call(
        write_kernel,
        name="write",
        out_shape=tuple(jax.ShapeDtypeStruct((layers, rows, columns), f32) for _ in range(4)),
        in_specs=[vmem, vmem],
        out_specs=(anywhere,) * 4,
        scratch_shapes=[pltpu.VMEM((4, layers, 2, rows, 128), f32), dma((4, layers, 2))],
        compiler_params=pltpu.CompilerParams(vmem_limit_bytes=40 << 20),
    )(blocks, strips)


def solution(mesh):
    placed = P(None, "lat", "lon")
    return jax.shard_map(
        functools.partial(local, mesh.shape["lon"], mesh.shape["lat"]),
        mesh=mesh,
        in_specs=(placed,) * 5,
        out_specs=(placed,) * 4,
        check_vma=False,
    )
```

time: 146 us -> 41.4 us (0.28)
  Pallas kernels: 145 us -> 40 us
    pallas_call x1, Pallas kernels: 104 us -> 36.8 us  [local(): pl.pallas_call(functools.partial(advance_kernel, lon_count, lat_count), n...]
    pallas_call x1, Pallas kernels: 40.9 us -> 3.18 us  [local(): pl.pallas_call(write_kernel, name='write', out_shape=tuple((jax.ShapeDtyp...]
where the time goes in v2:
time: 41.4 us; the launch traced here: 40.7 us
  Pallas kernels  40 us (97%)
  between operations  0.64 us (2%)
    pallas_call x1, Pallas kernels, local(): pl.pallas_call(functools.partial(advance_kernel, lon_count, lat_count), n...  36.8 us
    pallas_call x1, Pallas kernels, local(): pl.pallas_call(write_kernel, name='write', out_shape=tuple((jax.ShapeDtyp...  3.18 us

profile of v2, /device:TPU:27, one launch (start us, length us, event | category | flops | bytes accessed | tf_op | source)
XLA Modules:
  0.0 40.7 jit_solution(7153264025907894421)
XLA Ops:
  0.6 36.8 %advance.1 = (f32[4,6,2,208,128]{4,3,2,1,0:T(8,128)S(1)}, f32[4,208,128]{2,1,0:T(8,128)S(1)}) custom-call(f32[6,192,256]{2,1,0:T(8,128)} %t_ref.1, f32[6,192,256]{2,1,0:T(8,128)} %s_ref.1, f32[6,192,256]{2,1,0:T(8,128)} %u_ref.1, f32[6,192,256]{2,1,0:T(8,128)} %v_ref.1, s32[6,192,256]{2,1,0:T(8,128)} %w_ref.1), custom_call_target="tpu_custom_call" | custom-call | tf_op jit(solution)/shard_map/advance/pallas_call | solution.py:541
  37.5 3.2 %write.1 = (f32[6,192,256]{2,1,0:T(8,128)}, f32[6,192,256]{2,1,0:T(8,128)}, f32[6,192,256]{2,1,0:T(8,128)}, f32[6,192,256]{2,1,0:T(8,128)}) custom-call(f32[4,6,2,208,128]{4,3,2,1,0:T(8,128)S(1)} %get-tuple-element.6.blocks, f32[4,208,128]{2,1,0:T(8,128)S(1)} %get-tuple-element.7.strips), custom_call_target="tpu_custom_call" | custom-call | tf_op jit(solution)/shard_map/write/pallas_call | solution.py:575

commit v3 on v2

v3 whole, which is shorter than its diff:
```python
import functools

import jax
import jax.numpy as jnp
from jax import lax
from jax.experimental import pallas as pl
from jax.experimental.pallas import tpu as pltpu
from jax.sharding import PartitionSpec as P

MESH = pl.DeviceIdType.MESH
SCALE = 0.2 / 6.0
PITCH = 20
CHUNKS = 4
EARLY = 2
MIDDLE = 4
BLOCKS = 12
EDGES = 6
STRIPS = 25
JOINED = 13
WRITTEN = 12


def lanes():
    return lax.broadcasted_iota(jnp.int32, (8, 128), 1)


def spot():
    return lax.rem(lax.rem(lanes() + 4, 128), PITCH)


def roll(x, shift):
    shift = shift % 128 if isinstance(shift, int) else shift
    return x if isinstance(shift, int) and shift == 0 else pltpu.roll(x, shift, 1)


def shifted(values, distance):
    moved = [roll(value, -distance) for value in values]
    if len(moved) == 1:
        return moved
    first, second = moved
    if distance > 0:
        return [jnp.where(lanes() < 128 - distance, first, second), second]
    return [first, jnp.where(lanes() >= -distance, second, first)]


def face(weight, positive, before, here, after, beyond):
    near = jnp.where(positive, here, after)
    far = jnp.where(positive, before, beyond)
    return weight * (2.0 * (here + after) + (3.0 * near - far))


def staggered(items, stages, lag):
    held = [None] * len(items)
    for step in range(len(items) + lag * (len(stages) - 1)):
        for number, stage in enumerate(stages):
            at = step - lag * number
            if 0 <= at < len(items):
                held[at] = stage(items[at], held[at])


def tiles_step(tiles, lag):
    made = {}

    def shifts(item, _):
        number, k = item
        load, east_faces, _, _, _, late = tiles[number]
        here = load(k, 0)
        fields = shifted(here, -1), here, shifted(here, 1), shifted(here, 2)
        if k == 0:
            made[number, 0] = east_faces()
        if k == 2:
            made[number, 2] = fields[2] if late else here
        return fields

    def east(item, fields):
        number, k = item
        if k == 0:
            weight = [q * s for q, s in zip(made[number, 2], made[number, 0])]
            made[number, 0] = weight, [q > 0.0 for q in weight]
        flux = [face(*values) for values in zip(*made[number, 0], *fields)]
        return flux, shifted(flux, -1)

    def north(item, changes):
        number, k = item
        load, _, north_faces, south, put, late = tiles[number]
        if k == 0:
            weight = [q * s for q, s in zip(load(3, 1 if late else 0), north_faces())]
            made[number, 0] = weight, [q > 0.0 for q in weight]
        here = load(k, 0)
        flux = [face(*values) for values in zip(*made[number, 0], load(k, -1), here, load(k, 1), load(k, 2))]
        parts = zip(here, *changes, flux, south(k, flux), load(4, 0))
        put(k, [(q - ((e - w) + (n - m))) * s for q, e, w, n, m, s in parts])

    staggered([(number, k) for number in range(len(tiles)) for k in range(4)], (shifts, east, north), lag)


def rolled_south(k, flux):
    return [pltpu.roll(value, 1, 0) for value in flux]


def wet_east(load):
    here = load(4, 0)
    return [w * e * SCALE for w, e in zip(here, shifted(here, 1))]


def wet_north(load):
    return [w * n * SCALE for w, n in zip(load(4, 0), load(4, 1))]


def local_position():
    return lax.axis_index("lon"), lax.axis_index("lat")


def advance_kernel(
    lon_count,
    lat_count,
    t_ref,
    s_ref,
    u_ref,
    v_ref,
    w_ref,
    out,
    strips_out,
    x0,
    x1,
    wet_int,
    east_wet,
    north_wet,
    rows_in,
    wet_rows_in,
    packed,
    packed_next,
    wires,
    wires_in,
    strip,
    strip_mid,
    strip_next,
    flows,
    strip_flows,
    load_sem,
    row_send,
    row_recv,
    wire_send,
    wire_recv,
):
    inputs = (t_ref, s_ref, u_ref, v_ref, w_ref)
    layers, rows, _ = t_ref.shape
    north_pad = 8 + rows
    lon, lat = local_position()
    top = lat == lat_count - 1
    bottom = lat == 0
    east = {"lon": lax.rem(lon + 1, lon_count)}
    west = {"lon": lax.rem(lon + lon_count - 1, lon_count)}
    mirror = {"lon": lon_count - 1 - lon}

    part = rows // CHUNKS

    def loads(chunk):
        first = pl.multiple_of(part * chunk, 8)
        copies = []
        for k in (4, 0, 1, 2, 3):
            for half in range(2):
                here = inputs[k].at[:, pl.ds(first, part), pl.ds(128 * half, 128)]
                if k == 4:
                    there = wet_int.at[:, half, pl.ds(first, part)]
                else:
                    there = x0.at[k, :, half, pl.ds(pl.multiple_of(first + 8, 8), part)]
                copies.append(pltpu.make_async_copy(here, there, load_sem.at[chunk, k, half]))
        return copies

    @pl.loop(0, CHUNKS)
    def _(chunk):
        for copy in loads(chunk):
            copy.start()

    barrier = pltpu.get_barrier_semaphore()
    pl.semaphore_signal(barrier, inc=1, device_id=east, device_id_type=MESH)
    pl.semaphore_signal(barrier, inc=1, device_id=west, device_id_type=MESH)

    @pl.when(top)
    def _():
        pl.semaphore_signal(barrier, inc=1, device_id=mirror, device_id_type=MESH)

    @pl.when(jnp.logical_not(top))
    def _():
        pl.semaphore_signal(barrier, inc=1, device_id={"lat": lat + 1}, device_id_type=MESH)

    @pl.when(jnp.logical_not(bottom))
    def _():
        pl.semaphore_signal(barrier, inc=1, device_id={"lat": lat - 1}, device_id_type=MESH)

    def row_copies(first, there, side, device):
        copies = []
        for k in range(5):
            for half in range(2):
                source = inputs[k].at[:, pl.ds(first, 4), pl.ds(128 * half, 128)]
                if k == 4:
                    target = wet_rows_in.at[side, :, half, pl.ds(there, 4)]
                else:
                    target = rows_in.at[side, k, :, half, pl.ds(there, 4)]
                up = 0 if first else 1
                copies.append(
                    pltpu.make_async_remote_copy(
                        source,
                        target,
                        row_send.at[up, k, half],
                        row_recv.at[side, k, half],
                        device_id=device,
                        device_id_type=MESH,
                    )
                )
        return copies

    to_north = row_copies(rows - 4, 4, 0, {"lat": jnp.minimum(lat + 1, lat_count - 1)})
    to_mirror = row_copies(rows - 4, 4, 1, mirror)
    to_south = row_copies(0, 0, 1, {"lat": jnp.maximum(lat - 1, 0)})

    def pack_moves(source):
        return [roll(jnp.where(lanes() < 64, source(layer, 0), source(layer, 1)), PITCH * layer) for layer in range(layers)]

    def pack(moves):
        place = lax.rem(lanes() + 4, 128)
        total = moves[-1]
        for layer in reversed(range(layers - 1)):
            total = jnp.where(place < PITCH * (layer + 1) - 6, moves[layer], total)
        return jnp.where(place < 120, total, moves[0])

    def pack_tiles(starts):
        group = spot() // 4
        group_west = lax.rem(lanes(), PITCH) // 4
        made = {}

        def move(item, _):
            row, k = item
            return pack_moves(lambda layer, half: x0[k, layer, half, pl.ds(row, 8), :])

        def merge(item, moves):
            row, k = item
            one = pack(moves)
            packed[k, pl.ds(row, 8), :] = one
            return roll(one, 4 * k)

        def send(item, moved):
            row, k = item
            if k == 0:
                made["east"] = made["west"] = moved
            made["east"] = jnp.where(group == k, moved, made["east"])
            made["west"] = jnp.where(group_west == k, moved, made["west"])
            if k == 4:
                wires[0, pl.ds(row, 8), :] = made["east"]
                wires[1, pl.ds(row, 8), :] = made["west"]

        staggered([(row, k) for row in starts for k in range(5)], (move, merge, send), 3)

    def wire_copies(start, count, number):
        return [
            pltpu.make_async_remote_copy(
                wires.at[side, pl.ds(start, count)],
                wires_in.at[side, pl.ds(start, count)],
                wire_send.at[side, number],
                wire_recv.at[side, number],
                device_id=device,
                device_id_type=MESH,
            )
            for side, device in ((0, east), (1, west))
        ]

    tiles = rows // 8

    @pl.loop(0, CHUNKS)
    def _(chunk):
        for copy in loads(chunk):
            copy.wait()
        first = pl.multiple_of(part * chunk, 8)
        for layer in range(layers):
            for half in range(2):
                wet = wet_int[layer, half, pl.ds(first, part), :]
                x0[4, layer, half, pl.ds(pl.multiple_of(first + 8, 8), part), :] = wet.astype(jnp.float32)
        pack_tiles([pl.multiple_of(first + 8 + 8 * j, 8) for j in range(part // 8)])

    def loader(source, layer, first):
        def load(k, offset):
            at = pl.ds(first + offset, 8)
            return [(x0 if k == 4 else source)[k, layer, half, at, :] for half in range(2)]

        return load

    def face_weights(load, layer, first, first_step):
        at = pl.ds(first, 8)

        def faces(kept, make):
            if not first_step:
                return [kept[layer, half, at, :] for half in range(2)]
            values = make(load)
            for half in range(2):
                kept[layer, half, at, :] = values[half]
            return values

        return functools.partial(faces, east_wet, wet_east), functools.partial(faces, north_wet, wet_north)

    def whole_blocks(source, target, first_step, meanwhile):
        def tile(layer, first):
            at = pl.ds(first, 8)

            def south(k, flux):
                for half in range(2):
                    flows[k, half, at, :] = flux[half]
                return [flows[k, half, pl.ds(first - 1, 8), :] for half in range(2)]

            def put(k, new):
                for half in range(2):
                    target[k, layer, half, at, :] = new[half]

            load = loader(source, layer, first)
            return load, *face_weights(load, layer, first, first_step), south, put, False

        @pl.loop(0, layers)
        def _(layer):
            for before, function in meanwhile:
                pl.when(layer == before)(function)

            @pl.loop(0, rows // (8 * BLOCKS))
            def _(i):
                first = pl.multiple_of(8 + 8 * BLOCKS * i, 8)
                tiles_step([tile(layer, pl.multiple_of(first + 8 * j, 8)) for j in range(BLOCKS)], 12)

    sublane = lax.broadcasted_iota(jnp.int32, (8, 128), 0)

    def edge_rows(source, target, starts, first_step):
        right = jnp.logical_and(sublane >= 2, sublane < 6)

        def tile(layer, first):
            at = pl.ds(first, 8)

            def put(k, new):
                for half in range(2):
                    target[k, layer, half, at, :] = jnp.where(right, new[half], target[k, layer, half, at, :])

            load = loader(source, layer, first)
            return load, *face_weights(load, layer, first, first_step), rolled_south, put, False

        @pl.loop(0, layers // EDGES)
        def _(i):
            tiles_step([tile(EDGES * i + j, first) for j in range(EDGES) for first in starts], 12)

    past_fold = jnp.logical_and(sublane >= 4, sublane < 6)

    def fold_rows():
        first = north_pad - 4

        def tile(layer):
            at = pl.ds(first, 8)

            def put(k, new):
                for half in range(2):
                    x1[k, layer, half, at, :] = jnp.where(past_fold, new[half], x1[k, layer, half, at, :])

            load = loader(x0, layer, first)
            return load, lambda: wet_east(load), lambda: wet_north(load), rolled_south, put, True

        tiles_step([tile(layer) for layer in range(layers)], 12)

    def send_edges():
        @pl.when(bottom)
        def _():
            pl.semaphore_wait(barrier, 3)

        @pl.when(jnp.logical_not(bottom))
        def _():
            pl.semaphore_wait(barrier, 4)

        @pl.when(top)
        def _():
            for copy in to_mirror:
                copy.start()

        @pl.when(jnp.logical_not(top))
        def _():
            for copy in to_north:
                copy.start()

        @pl.when(jnp.logical_not(bottom))
        def _():
            for copy in to_south:
                copy.start()

        for copy in wire_copies(8, rows, 0):
            copy.start()

    whole_blocks(x0, x1, True, [(EARLY, send_edges)])

    @pl.when(bottom)
    def _():
        @pl.loop(0, layers)
        def _(layer):
            for half in range(2):
                for k in range(5):
                    x0[k, layer, half, pl.ds(0, 8), :] = jnp.zeros((8, 128), jnp.float32)

    @pl.when(jnp.logical_not(bottom))
    def _():
        for copy in row_copies(0, 4, 0, east):
            copy.wait_recv()

        @pl.loop(0, layers)
        def _(layer):
            for half in range(2):
                for k in range(4):
                    x0[k, layer, half, pl.ds(0, 8), :] = rows_in[0, k, layer, half]
                x0[4, layer, half, pl.ds(0, 8), :] = wet_rows_in[0, layer, half].astype(jnp.float32)

    def send_corner(number, start):
        pack_tiles([start])
        for copy in wire_copies(start, 8, number):
            copy.start()

    send_corner(1, 0)

    def north_tile(k, layer, half):
        return wet_rows_in[1, layer, half].astype(jnp.float32) if k == 4 else rows_in[1, k, layer, half]

    @pl.when(jnp.logical_not(top))
    def _():
        for copy in to_south:
            copy.wait_recv()

        @pl.loop(0, layers)
        def _(layer):
            for half in range(2):
                for k in range(5):
                    x0[k, layer, half, pl.ds(north_pad, 8), :] = north_tile(k, layer, half)

        send_corner(2, north_pad)

    def fold_halo():
        @pl.when(top)
        def _():
            for copy in to_south:
                copy.wait_recv()

            @pl.loop(0, layers)
            def _(layer):
                for half in range(2):
                    for k in range(5):
                        flipped = jnp.take_along_axis(north_tile(k, layer, 1 - half), 127 - lanes(), axis=1)
                        if k in (2, 3):
                            flipped = -flipped
                        for row in range(4):
                            x0[k, layer, half, pl.ds(north_pad + row, 1), :] = flipped[7 - row : 8 - row, :]

            send_corner(2, north_pad)

    whole_blocks(x1, out, False, [(MIDDLE, fold_halo)])
    wire_parts = wire_copies(8, rows, 0) + wire_copies(0, 8, 1) + wire_copies(north_pad, 8, 2)
    edge_rows(x0, x1, (4, north_pad - 4), True)
    pl.when(top)(fold_rows)
    edge_rows(x1, out, (6, north_pad - 6), False)

    def every_tile(*stages):
        @pl.loop(0, (tiles + 2) // JOINED)
        def _(i):
            at = [pl.ds(pl.multiple_of(8 * JOINED * i + 8 * j, 8), 8) for j in range(JOINED)]
            staggered([(tile, k) for tile in at for k in range(5)], stages, 8)

    def move_next(item, _):
        tile, k = item
        source = x0 if k == 4 else x1
        return pack_moves(lambda layer, half: source[k, layer, half, tile, :])

    def merge_next(item, moves):
        tile, k = item
        packed_next[k, tile, :] = pack(moves)

    every_tile(move_next, merge_next)

    for copy in wire_parts:
        copy.wait_recv()

    def join(item, _):
        tile, k = item
        own = packed[k, tile, :]
        return roll(wires_in[0, tile, :], -4 * k), own, roll(own, 8), roll(wires_in[1, tile, :], 8 - 4 * k)

    def select(parts):
        place = spot()
        left = jnp.where(place < 4, parts[0], parts[1])
        right = jnp.where(place < 12, parts[2], parts[3])
        return jnp.where(place < 8, left, right)

    def put_strip(item, parts):
        tile, k = item
        strip[k, tile, :] = select(parts)

    every_tile(join, put_strip)

    def strip_tile(source, first, put, south=None, late=False):
        def load(k, offset):
            return [source[k, pl.ds(first + offset, 8), :]]

        def stored(k, flux):
            strip_flows[k, pl.ds(first, 8), :] = flux[0]
            return [strip_flows[k, pl.ds(first - 1, 8), :]]

        made = lambda: wet_east(load), lambda: wet_north(load)
        return load, *made, south or stored, functools.partial(put, first), late

    def strip_step(source, put):
        @pl.loop(0, (tiles + 1) // STRIPS)
        def _(i):
            first = 4 + 8 * STRIPS * i
            tiles_step([strip_tile(source, first + 8 * j, put) for j in range(STRIPS)], 20)

    def put_mid(first, k, new):
        strip_mid[k, pl.ds(first, 8), :] = new[0]

    strip_step(strip, put_mid)

    @pl.when(top)
    def _():
        def put(first, k, new):
            at = pl.ds(first, 8)
            strip_mid[k, at, :] = jnp.where(past_fold, new[0], strip_mid[k, at, :])

        tiles_step([strip_tile(strip, north_pad - 4, put, rolled_south, True)], 4)

    def join_next(item, _):
        tile, k = item
        outer = strip[4, tile, :] if k == 4 else strip_mid[k, tile, :]
        inner = packed_next[k, tile, :]
        return roll(outer, -2), roll(inner, -2), roll(inner, 10), roll(outer, 2)

    def put_strip_next(item, parts):
        tile, k = item
        strip_next[k, tile, :] = select(parts)

    every_tile(join_next, put_strip_next)

    def put_out(first, k, new):
        place = spot()
        inside = jnp.logical_and(place >= 2, place < 6)
        strips_out[k, pl.ds(first, 8), :] = jnp.where(inside, new[0], roll(new[0], -12))

    strip_step(strip_next, put_out)

    for copy in wire_parts:
        copy.wait_send()
    for copy in to_mirror:
        copy.wait_send()

    @pl.when(jnp.logical_not(bottom))
    def _():
        for copy in to_south:
            copy.wait_send()


def write_kernel(blocks, strips, t_out, s_out, u_out, v_out, whole, sem):
    layers, rows, _ = t_out.shape
    copies = []
    for k, output in enumerate((t_out, s_out, u_out, v_out)):

        @pl.loop(0, rows // (8 * WRITTEN))
        def _(i):
            first = pl.multiple_of(8 * WRITTEN * i, 8)

            def move(start, _):
                strip = strips[k, pl.ds(start + 8, 8), :]
                return [roll(strip, 2 - PITCH * layer) for layer in range(layers)]

            def merge(start, moved):
                for layer in range(layers):
                    for half in range(2):
                        edge = lanes() < 4 if half == 0 else lanes() >= 124
                        block = blocks[k, layer, half, pl.ds(start + 8, 8), :]
                        whole[k, layer, half, pl.ds(start, 8), :] = jnp.where(edge, moved[layer], block)

            staggered([pl.multiple_of(first + 8 * j, 8) for j in range(WRITTEN)], (move, merge), 5)

        for layer in range(layers):
            for half in range(2):
                there = output.at[layer, :, pl.ds(128 * half, 128)]
                copy = pltpu.make_async_copy(whole.at[k, layer, half], there, sem.at[k, layer, half])
                copy.start()
                copies.append(copy)
    for copy in copies:
        copy.wait()


def local(lon_count, lat_count, *arrays):
    layers, rows, columns = arrays[0].shape
    padded = rows + 16
    vmem = pl.BlockSpec(memory_space=pltpu.VMEM)
    anywhere = pl.BlockSpec(memory_space=pltpu.HBM)
    dma = pltpu.SemaphoreType.DMA
    f32 = jnp.float32
    blocks, strips = pl.pallas_call(
        functools.partial(advance_kernel, lon_count, lat_count),
        name="advance",
        out_shape=(
            jax.ShapeDtypeStruct((4, layers, 2, padded, 128), f32),
            jax.ShapeDtypeStruct((4, padded, 128), f32),
        ),
        in_specs=[anywhere] * 5,
        out_specs=(vmem, vmem),
        scratch_shapes=[
            pltpu.VMEM((5, layers, 2, padded, 128), f32),
            pltpu.VMEM((4, layers, 2, padded, 128), f32),
            pltpu.VMEM((layers, 2, rows, 128), jnp.int32),
            pltpu.VMEM((layers, 2, padded, 128), f32),
            pltpu.VMEM((layers, 2, padded, 128), f32),
            pltpu.VMEM((2, 4, layers, 2, 8, 128), f32),
            pltpu.VMEM((2, layers, 2, 8, 128), jnp.int32),
            pltpu.VMEM((5, padded, 128), f32),
            pltpu.VMEM((5, padded, 128), f32),
            pltpu.VMEM((2, padded, 128), f32),
            pltpu.VMEM((2, padded, 128), f32),
            pltpu.VMEM((5, padded, 128), f32),
            pltpu.VMEM((4, padded, 128), f32),
            pltpu.VMEM((5, padded, 128), f32),
            pltpu.VMEM((4, 2, padded, 128), f32),
            pltpu.VMEM((4, padded, 128), f32),
            dma((CHUNKS, 5, 2)),
            dma((2, 5, 2)),
            dma((2, 5, 2)),
            dma((2, 3)),
            dma((2, 3)),
        ],
        compiler_params=pltpu.CompilerParams(collective_id=0, has_side_effects=True, vmem_limit_bytes=40 << 20),
    )(*(pltpu.with_memory_space_constraint(array, pltpu.HBM) for array in arrays))
    return pl.pallas_call(
        write_kernel,
        name="write",
        out_shape=tuple(jax.ShapeDtypeStruct((layers, rows, columns), f32) for _ in range(4)),
        in_specs=[vmem, vmem],
        out_specs=(anywhere,) * 4,
        scratch_shapes=[pltpu.VMEM((4, layers, 2, rows, 128), f32), dma((4, layers, 2))],
        compiler_params=pltpu.CompilerParams(vmem_limit_bytes=40 << 20),
    )(blocks, strips)


def solution(mesh):
    placed = P(None, "lat", "lon")
    return jax.shard_map(
        functools.partial(local, mesh.shape["lon"], mesh.shape["lat"]),
        mesh=mesh,
        in_specs=(placed,) * 5,
        out_specs=(placed,) * 4,
        check_vma=False,
    )
```

time: 41.4 us -> 30.5 us (0.74)
  Pallas kernels: 40 us -> 29.5 us
    pallas_call x1, Pallas kernels: 36.8 us -> 26.6 us  [local(): pl.pallas_call(functools.partial(advance_kernel, lon_count, lat_count), n...]
where the time goes in v3:
time: 30.5 us; the launch traced here: 30.1 us
  Pallas kernels  29.5 us (97%)
  between operations  0.64 us (2%)
    pallas_call x1, Pallas kernels, local(): pl.pallas_call(functools.partial(advance_kernel, lon_count, lat_count), n...  26.6 us
    pallas_call x1, Pallas kernels, local(): pl.pallas_call(write_kernel, name='write', out_shape=tuple((jax.ShapeDtyp...  2.87 us

profile of v3, /device:TPU:27, one launch (start us, length us, event | category | flops | bytes accessed | tf_op | source)
XLA Modules:
  0.0 30.1 jit_solution(2393413669947788567)
XLA Ops:
  0.6 26.6 %advance.1 = (f32[4,6,2,208,128]{4,3,2,1,0:T(8,128)S(1)}, f32[4,208,128]{2,1,0:T(8,128)S(1)}) custom-call(f32[6,192,256]{2,1,0:T(8,128)} %t_ref.1, f32[6,192,256]{2,1,0:T(8,128)} %s_ref.1, f32[6,192,256]{2,1,0:T(8,128)} %u_ref.1, f32[6,192,256]{2,1,0:T(8,128)} %v_ref.1, s32[6,192,256]{2,1,0:T(8,128)} %w_ref.1), custom_call_target="tpu_custom_call" | custom-call | tf_op jit(solution)/shard_map/advance/pallas_call | solution.py:595
  27.3 2.9 %write.1 = (f32[6,192,256]{2,1,0:T(8,128)}, f32[6,192,256]{2,1,0:T(8,128)}, f32[6,192,256]{2,1,0:T(8,128)}, f32[6,192,256]{2,1,0:T(8,128)}) custom-call(f32[4,6,2,208,128]{4,3,2,1,0:T(8,128)S(1)} %get-tuple-element.6.blocks, f32[4,208,128]{2,1,0:T(8,128)S(1)} %get-tuple-element.7.strips), custom_call_target="tpu_custom_call" | custom-call | tf_op jit(solution)/shard_map/write/pallas_call | solution.py:629

commit v4 on v3

--- a/solution.py
+++ b/solution.py
@@ -11,9 +11,10 @@
 SCALE = 0.2 / 6.0
 PITCH = 20
 CHUNKS = 4
-EARLY = 2
-MIDDLE = 4
-BLOCKS = 12
+EARLY = 1
+LATER = 2
+MIDDLE = 2
+BLOCKS = 24
 EDGES = 6
 STRIPS = 25
 JOINED = 13
@@ -360,7 +361,7 @@
 
         tiles_step([tile(layer) for layer in range(layers)], 12)
 
-    def send_edges():
+    def send_rows():
         @pl.when(bottom)
         def _():
             pl.semaphore_wait(barrier, 3)
@@ -384,10 +385,11 @@
             for copy in to_south:
                 copy.start()
 
+    def send_wires():
         for copy in wire_copies(8, rows, 0):
             copy.start()
 
-    whole_blocks(x0, x1, True, [(EARLY, send_edges)])
+    whole_blocks(x0, x1, True, [(EARLY, send_rows), (LATER, send_wires)])
 
     @pl.when(bottom)
     def _():

time: 30.5 us -> 29.9 us (0.980)
    pallas_call x1, Pallas kernels: 26.6 us -> 26.3 us  [local(): pl.pallas_call(functools.partial(advance_kernel, lon_count, lat_count), n...]
where the time goes in v4:
time: 29.9 us; the launch traced here: 29.8 us
  Pallas kernels  29.2 us (98%)
  between operations  0.64 us (2%)
    pallas_call x1, Pallas kernels, local(): pl.pallas_call(functools.partial(advance_kernel, lon_count, lat_count), n...  26.3 us
    pallas_call x1, Pallas kernels, local(): pl.pallas_call(write_kernel, name='write', out_shape=tuple((jax.ShapeDtyp...  2.87 us

profile of v4, /device:TPU:27, one launch (start us, length us, event | category | flops | bytes accessed | tf_op | source)
XLA Modules:
  0.0 29.8 jit_solution(8181870573449130054)
XLA Ops:
  0.6 26.3 %advance.1 = (f32[4,6,2,208,128]{4,3,2,1,0:T(8,128)S(1)}, f32[4,208,128]{2,1,0:T(8,128)S(1)}) custom-call(f32[6,192,256]{2,1,0:T(8,128)} %t_ref.1, f32[6,192,256]{2,1,0:T(8,128)} %s_ref.1, f32[6,192,256]{2,1,0:T(8,128)} %u_ref.1, f32[6,192,256]{2,1,0:T(8,128)} %v_ref.1, s32[6,192,256]{2,1,0:T(8,128)} %w_ref.1), custom_call_target="tpu_custom_call" | custom-call | tf_op jit(solution)/shard_map/advance/pallas_call | solution.py:597
  26.9 2.9 %write.1 = (f32[6,192,256]{2,1,0:T(8,128)}, f32[6,192,256]{2,1,0:T(8,128)}, f32[6,192,256]{2,1,0:T(8,128)}, f32[6,192,256]{2,1,0:T(8,128)}) custom-call(f32[4,6,2,208,128]{4,3,2,1,0:T(8,128)S(1)} %get-tuple-element.6.blocks, f32[4,208,128]{2,1,0:T(8,128)S(1)} %get-tuple-element.7.strips), custom_call_target="tpu_custom_call" | custom-call | tf_op jit(solution)/shard_map/write/pallas_call | solution.py:631
